TPU v7x, 512 devices: a whole 4x4x16 slice. The times are simulated.
512 devices in a mesh: row: 32 (over z_lo, y, core), col: 16 (over x, z_hi).
Axes of the slice: x: 4, y: 4, z: 16 (z_hi: 4, z_lo: 4; z = z_hi * 4 + z_lo), core: 2. Of those that a mesh axis runs over, the one named last changes fastest.
Arguments:
- row_cells: int32 [3, 32768], P(None, 'row'), may hold values from 0 to 63
- col_cells: int32 [3, 131072], P(None, 'col'), may hold values from 0 to 63
- omega: float32 [16, 131072], P(None, 'col'), may hold values from -6 to 6
Outputs:
- basis: float32 [16, 32768], P(None, 'row')
- image: float32 [16, 131072], P(None, 'col')
- core: float32 [16, 16], replicated
All inputs are finite; a program needn't handle non-finite values.
Results may differ from a plain program's by a relative error of at most 0.0001.
Values sent between devices are 32-bit elements; how exact they have to be, the bound alone decides.
No kernel may reach another device: no remote copies, remote signals or barrier semaphores. Data moves between devices by JAX's collectives and lax.ppermute only.
A program may use at most 64 MiB of HBM per device.

v0:
```python
import jax
import jax.numpy as jnp
from jax import lax
from jax.sharding import Mesh
from jax.sharding import PartitionSpec as P

ROW = ("row_0", "row_1", "row_2")
COL = ("col_0", "col_1")
ROW_COL = ("row_0", "row_1", "row_2", "col_0", "col_1")


def sent_to_all(array, axis):
    copies = jnp.broadcast_to(array, (lax.axis_size(axis), *array.shape))
    return lax.all_to_all(copies, axis, split_axis=0, concat_axis=0, tiled=True)


def of_everyone(array, axis):
    return sent_to_all(array, axis).sum(axis=0)


def in_blocks(array, dim, length):
    before, after = (array.shape[:dim], array.shape[dim + 1 :])
    return jnp.moveaxis(array.reshape(*before, length, -1, *after), dim, 0)


def summed_on_arrival(array, axis, dim):
    parts = in_blocks(array, dim, lax.axis_size(axis))
    arrived = lax.all_to_all(parts, axis, split_axis=0, concat_axis=0, tiled=True)
    return arrived.sum(axis=0)


def over_axes(array, axes):
    for axis in axes:
        array = lax.psum(array, axis)
    return array


def joined_along(parts, dim):
    parts = jnp.moveaxis(parts, 0, dim)
    lengths = parts.shape
    return parts.reshape(*lengths[:dim], lengths[dim] * lengths[dim + 1], *lengths[dim + 2 :])


def gather_directly(array, axis, dim):
    return joined_along(sent_to_all(array, axis), dim)


def kernel_tile(rows, cols):
    first = (rows[0][:, None] - cols[0][None, :]).astype(jnp.float32)
    total = first * first
    second = (rows[1][:, None] - cols[1][None, :]).astype(jnp.float32)
    total = total + second * second
    third = (rows[2][:, None] - cols[2][None, :]).astype(jnp.float32)
    total = total + third * third
    return 0.25 * jnp.exp(-jnp.sqrt(total) / 6.4)


def shards(row_cells, col_cells, omega):
    rank = omega.shape[0]
    local_rows = row_cells.shape[1]
    local_cols = col_cells.shape[1]
    rows_total = local_rows * lax.axis_size(ROW)
    order = local_cols * lax.axis_size(COL)
    width = min(local_cols, 2048)
    count = local_cols // width

    def tile_at(index):
        cols = lax.dynamic_slice_in_dim(col_cells, index * width, width, 1)
        return kernel_tile(row_cells, cols)

    def sketch_step(index, total):
        tests = lax.dynamic_slice_in_dim(omega, index * width, width, 1)
        return total + lax.dot_general(
            tests, tile_at(index), (((1,), (1,)), ((), ())), precision=lax.Precision.HIGHEST
        )

    sketch_part = lax.fori_loop(0, count, sketch_step, jnp.zeros((rank, local_rows), jnp.float32))
    sketch = of_everyone(sketch_part, COL)
    gram = of_everyone(jnp.dot(sketch, sketch.T, precision=lax.Precision.HIGHEST), ROW) / rows_total
    lower = jnp.linalg.cholesky(gram)
    basis = jax.scipy.linalg.solve_triangular(lower, sketch, lower=True)

    def image_step(index, total):
        piece = jnp.dot(basis, tile_at(index), precision=lax.Precision.HIGHEST)
        return lax.dynamic_update_slice_in_dim(total, piece, index * width, 1)

    image_part = lax.fori_loop(0, count, image_step, jnp.zeros((rank, local_cols), jnp.float32))
    image_share = summed_on_arrival(image_part, ROW, 1)
    core = (
        over_axes(jnp.dot(image_share, image_share.T, precision=lax.Precision.HIGHEST), ROW_COL)
        / order
    )
    image = gather_directly(image_share, ROW, 1)
    return (basis, image, core)


def solution(mesh):
    finer = Mesh(mesh.devices.reshape(4, 4, 2, 4, 4), ("row_0", "row_1", "row_2", "col_0", "col_1"))
    return jax.shard_map(
        shards,
        mesh=finer,
        in_specs=(P(None, ROW), P(None, COL), P(None, COL)),
        out_specs=(P(None, ROW), P(None, COL), P()),
        check_vma=False,
    )
```

profile of v0, /device:TPU:1, one launch (start us, length us, event | category | flops | bytes accessed | tf_op | source)
XLA Modules:
  0.0 274.6 jit_solution(13617429852910083274)
XLA Ops:
  0.6 60.1 %while.28 = (s32[]{:T(128)}, f32[16,1024]{1,0:T(8,128)S(1)}, f32[16,8192]{1,0:T(8,128)}, s32[3,1024]{1,0:T(4,128)}, s32[3,8192]{1,0:T(4,128)}, /*index=5*/s32[]{...) while((s32[]{:T(128)}, f32[16,1024]{1,0:T(8,128)S(1)}, f32[16,8192]{1,0:T(8,128)}, ...), condition=%wide.region_1.0_spmd.clone, body=%wide.region_0.0_spmd.clone.sunk | while | flops 432046080 | bytes 372941 | solution.py:77
  0.7 1.0 constant_dynamic-slice_fusion.5
  2.5 13.2 %fusion.94 = f32[16,1024]{1,0:T(8,128)S(1)} fusion(s32[2048]{0:T(1024)S(1)} %bitcast.72, s32[1024]{0:T(1024)S(1)} %bitcast.77, s32[2048]{0:T(1024)S(1)} %bitcast.71, s32[1024]{0:T(1024)S(1)} %bitcast.78, s32[2048]{0:T(1024)S(1)} %bitcast.70, s32[1024]{0:T(1024)S(1)} %bitcast.76, f32[16,8192]{1,0:T(8,128)} %get-tuple-element.353, s32[]{:T(128)S(6)} %select_n.28, ...), kind=kOutput, calls=%fused_computation.55.clone.1 | convolution fusion | flops 432046080 | bytes 299013 | tf_op jit(solution)/shard_map/while/body/eval_jaxpr/dot_general | solution.py:73
  15.7 1.0 constant_dynamic-slice_fusion.5
  17.5 13.2 %fusion.94 = f32[16,1024]{1,0:T(8,128)S(1)} fusion(s32[2048]{0:T(1024)S(1)} %bitcast.72, s32[1024]{0:T(1024)S(1)} %bitcast.77, s32[2048]{0:T(1024)S(1)} %bitcast.71, s32[1024]{0:T(1024)S(1)} %bitcast.78, s32[2048]{0:T(1024)S(1)} %bitcast.70, s32[1024]{0:T(1024)S(1)} %bitcast.76, f32[16,8192]{1,0:T(8,128)} %get-tuple-element.353, s32[]{:T(128)S(6)} %select_n.28, ...), kind=kOutput, calls=%fused_computation.55.clone.1 | convolution fusion | flops 432046080 | bytes 299013 | tf_op jit(solution)/shard_map/while/body/eval_jaxpr/dot_general | solution.py:73
  32.5 13.2 %fusion.94 = f32[16,1024]{1,0:T(8,128)S(1)} fusion(s32[2048]{0:T(1024)S(1)} %bitcast.72, s32[1024]{0:T(1024)S(1)} %bitcast.77, s32[2048]{0:T(1024)S(1)} %bitcast.71, s32[1024]{0:T(1024)S(1)} %bitcast.78, s32[2048]{0:T(1024)S(1)} %bitcast.70, s32[1024]{0:T(1024)S(1)} %bitcast.76, f32[16,8192]{1,0:T(8,128)} %get-tuple-element.353, s32[]{:T(128)S(6)} %select_n.28, ...), kind=kOutput, calls=%fused_computation.55.clone.1 | convolution fusion | flops 432046080 | bytes 299013 | tf_op jit(solution)/shard_map/while/body/eval_jaxpr/dot_general | solution.py:73
  47.6 13.2 %fusion.94 = f32[16,1024]{1,0:T(8,128)S(1)} fusion(s32[2048]{0:T(1024)S(1)} %bitcast.72, s32[1024]{0:T(1024)S(1)} %bitcast.77, s32[2048]{0:T(1024)S(1)} %bitcast.71, s32[1024]{0:T(1024)S(1)} %bitcast.78, s32[2048]{0:T(1024)S(1)} %bitcast.70, s32[1024]{0:T(1024)S(1)} %bitcast.76, f32[16,8192]{1,0:T(8,128)} %get-tuple-element.353, s32[]{:T(128)S(6)} %select_n.28, ...), kind=kOutput, calls=%fused_computation.55.clone.1 | convolution fusion | flops 432046080 | bytes 299013 | tf_op jit(solution)/shard_map/while/body/eval_jaxpr/dot_general | solution.py:73
  60.9 68.0 %all_to_all.20 = f32[16,16,1024]{2,1,0:T(8,128)S(1)} all-to-all(f32[16,16,1024]{2,1,0:T(8,128)S(1)} %broadcast_in_dim.18), channel_id=1, replica_groups=mesh['row_0'=4,'row_1'=4,'row_2'=2,'col_0'=4,'col_1'=4] {'col_0','col_1'}, dimensions={0} | all-to-all | bytes 2097152 | tf_op jit(solution)/shard_map/all_to_all | solution.py:14
  130.0 13.9 %all-to-all-start.1 = ((f32[32,1,256]{2,1,0:T(1,128)}), f32[32,1,256]{2,1,0:T(1,128)S(1)}, u32[]{:S(2)}, u32[]{:S(2)}) async-start(f32[32,1,256]{2,1,0:T(1,128)} %reshape.30), calls=%async_computation.1 | async-start | bytes 65536 | tf_op jit(solution)/shard_map/all_to_all | solution.py:14
  143.9 7.6 %all-to-all-done.1 = f32[32,1,256]{2,1,0:T(1,128)S(1)} async-done(((f32[32,1,256]{2,1,0:T(1,128)}), f32[32,1,256]{2,1,0:T(1,128)S(1)}, u32[]{:S(2)}, u32[]{:S(2)}) %all-to-all-start.1) | async-done | bytes 32800 | tf_op jit(solution)/shard_map/all_to_all | solution.py:14
  153.0 1.5 cholesky.16
  155.8 1.2 custom-call.7
  157.3 45.4 %while.27 = (s32[]{:T(128)}, f32[16,8192]{1,0:T(8,128)S(1)}, s32[3,1024]{1,0:T(4,128)S(1)}, s32[3,8192]{1,0:T(4,128)}, f32[16,1024]{1,0:T(8,128)S(1)}, /*index=5...) while((s32[]{:T(128)}, f32[16,8192]{1,0:T(8,128)S(1)}, s32[3,1024]{1,0:T(4,128)S(1)}, ...), condition=%wide.region_7.8_spmd, body=%wide.region_6.7_spmd.sunk | while | flops 432013312 | bytes 307395 | solution.py:87
  158.4 10.3 %fusion.90 = f32[16,8192]{1,0:T(8,128)S(1)} fusion(f32[16,8192]{1,0:T(8,128)S(1)} %get-tuple-element.374, s32[]{:T(128)S(6)} %select_n.27, f32[16,1024]{1,0:T(8,128)S(1)} %get-tuple-element.388, s32[2048]{0:T(1024)S(1)} %bitcast.75, s32[1024]{0:T(1024)S(1)} %bitcast.80, s32[2048]{0:T(1024)S(1)} %bitcast.74, s32[1024]{0:T(1024)S(1)} %bitcast.81, ...), kind=kOutput, calls=%fused_computation.26.clone.1 | convolution fusion | flops 432013312 | bytes 233476 | tf_op jit(solution)/shard_map/while/body/eval_jaxpr/dot_general | solution.py:84
  169.7 10.3 %fusion.90 = f32[16,8192]{1,0:T(8,128)S(1)} fusion(f32[16,8192]{1,0:T(8,128)S(1)} %get-tuple-element.374, s32[]{:T(128)S(6)} %select_n.27, f32[16,1024]{1,0:T(8,128)S(1)} %get-tuple-element.388, s32[2048]{0:T(1024)S(1)} %bitcast.75, s32[1024]{0:T(1024)S(1)} %bitcast.80, s32[2048]{0:T(1024)S(1)} %bitcast.74, s32[1024]{0:T(1024)S(1)} %bitcast.81, ...), kind=kOutput, calls=%fused_computation.26.clone.1 | convolution fusion | flops 432013312 | bytes 233476 | tf_op jit(solution)/shard_map/while/body/eval_jaxpr/dot_general | solution.py:84
  181.0 10.3 %fusion.90 = f32[16,8192]{1,0:T(8,128)S(1)} fusion(f32[16,8192]{1,0:T(8,128)S(1)} %get-tuple-element.374, s32[]{:T(128)S(6)} %select_n.27, f32[16,1024]{1,0:T(8,128)S(1)} %get-tuple-element.388, s32[2048]{0:T(1024)S(1)} %bitcast.75, s32[1024]{0:T(1024)S(1)} %bitcast.80, s32[2048]{0:T(1024)S(1)} %bitcast.74, s32[1024]{0:T(1024)S(1)} %bitcast.81, ...), kind=kOutput, calls=%fused_computation.26.clone.1 | convolution fusion | flops 432013312 | bytes 233476 | tf_op jit(solution)/shard_map/while/body/eval_jaxpr/dot_general | solution.py:84
  192.4 10.3 %fusion.90 = f32[16,8192]{1,0:T(8,128)S(1)} fusion(f32[16,8192]{1,0:T(8,128)S(1)} %get-tuple-element.374, s32[]{:T(128)S(6)} %select_n.27, f32[16,1024]{1,0:T(8,128)S(1)} %get-tuple-element.388, s32[2048]{0:T(1024)S(1)} %bitcast.75, s32[1024]{0:T(1024)S(1)} %bitcast.80, s32[2048]{0:T(1024)S(1)} %bitcast.74, s32[1024]{0:T(1024)S(1)} %bitcast.81, ...), kind=kOutput, calls=%fused_computation.26.clone.1 | convolution fusion | flops 432013312 | bytes 233476 | tf_op jit(solution)/shard_map/while/body/eval_jaxpr/dot_general | solution.py:84
  203.3 19.5 %all_to_all.21 = f32[32,16,256]{2,1,0:T(8,128)S(1)} all-to-all(f32[32,16,256]{2,1,0:T(8,128)S(1)} %copy.16), channel_id=1, replica_groups=mesh['row_0'=4,'row_1'=4,'row_2'=2,'col_0'=4,'col_1'=4] {'row_0','row_1'..., dimensions={0} | all-to-all | bytes 1048576 | tf_op jit(solution)/shard_map/all_to_all | solution.py:28
  223.8 4.1 %all-to-all-start.3 = ((f32[32,16,256]{2,1,0:T(8,128)}), f32[32,16,256]{2,1,0:T(8,128)S(1)}, u32[]{:S(2)}, u32[]{:S(2)}) async-start(f32[32,16,256]{2,1,0:T(8,128)} %broadcast_in_dim.21), calls=%async_computation.3 | async-start | bytes 1048576 | tf_op jit(solution)/shard_map/all_to_all | solution.py:14
  228.0 14.3 %psum.35 = f32[16,16]{1,0:T(8,128)S(1)} all-reduce(f32[16,16]{1,0:T(8,128)S(1)} %fusion.72), channel_id=1, replica_groups=mesh['row_0'=4,'row_1'=4,'row_2'=2,'col_0'=4,'col_1'=4] {'row_0'}, use_global_device_ids=true, to_apply=%region_9.10 | all-reduce | flops 256 | bytes 2048 | tf_op jit(solution)/shard_map/psum | solution.py:34
  242.3 8.4 %psum.36 = f32[16,16]{1,0:T(8,128)S(1)} all-reduce(f32[16,16]{1,0:T(8,128)S(1)} %psum.35), channel_id=1, replica_groups=mesh['row_0'=4,'row_1'=4,'row_2'=2,'col_0'=4,'col_1'=4] {'row_1'}, use_global_device_ids=true, to_apply=%region_10.11 | all-reduce | flops 256 | bytes 2048 | tf_op jit(solution)/shard_map/psum | solution.py:34
  250.7 5.8 %psum.37 = f32[16,16]{1,0:T(8,128)S(1)} all-reduce(f32[16,16]{1,0:T(8,128)S(1)} %psum.36), channel_id=1, replica_groups=mesh['row_0'=4,'row_1'=4,'row_2'=2,'col_0'=4,'col_1'=4] {'row_2'}, use_global_device_ids=true, to_apply=%region_11.12 | all-reduce | flops 256 | bytes 2048 | tf_op jit(solution)/shard_map/psum | solution.py:34
  256.5 6.7 %psum.38 = f32[16,16]{1,0:T(8,128)S(1)} all-reduce(f32[16,16]{1,0:T(8,128)S(1)} %psum.37), channel_id=1, replica_groups=mesh['row_0'=4,'row_1'=4,'row_2'=2,'col_0'=4,'col_1'=4] {'col_0'}, use_global_device_ids=true, to_apply=%region_12.13 | all-reduce | flops 256 | bytes 2048 | tf_op jit(solution)/shard_map/psum | solution.py:34
  263.1 10.0 %psum.39 = f32[16,16]{1,0:T(8,128)S(1)} all-reduce(f32[16,16]{1,0:T(8,128)S(1)} %psum.38), channel_id=1, replica_groups=mesh['row_0'=4,'row_1'=4,'row_2'=2,'col_0'=4,'col_1'=4] {'col_1'}, use_global_device_ids=true, to_apply=%region_13.14 | all-reduce | flops 256 | bytes 2048 | tf_op jit(solution)/shard_map/psum | solution.py:34
  (43 shorter events, 16.6 us)
Async XLA Ops:
  128.9 28.4 %copy-start = (s32[3,1024]{1,0:T(4,128)S(1)}, s32[3,1024]{1,0:T(4,128)}, u32[]{:S(2)}) copy-start(s32[3,1024]{1,0:T(4,128)} %get-tuple-element.396) | copy-start | bytes 36868
  130.0 21.5 %all-to-all-start.1 = ((f32[32,1,256]{2,1,0:T(1,128)}), f32[32,1,256]{2,1,0:T(1,128)S(1)}, u32[]{:S(2)}, u32[]{:S(2)}) async-start(f32[32,1,256]{2,1,0:T(1,128)} %reshape.30), calls=%async_computation.1 | async-start | bytes 65536 | tf_op jit(solution)/shard_map/all_to_all | solution.py:14
  202.7 0.6 copy-start.1
  223.8 50.0 %all-to-all-start.3 = ((f32[32,16,256]{2,1,0:T(8,128)}), f32[32,16,256]{2,1,0:T(8,128)S(1)}, u32[]{:S(2)}, u32[]{:S(2)}) async-start(f32[32,16,256]{2,1,0:T(8,128)} %broadcast_in_dim.21), calls=%async_computation.3 | async-start | bytes 1048576 | tf_op jit(solution)/shard_map/all_to_all | solution.py:14
where the time goes:
time: 279 us; the launch traced here: 275 us
  blocking collectives  133 us (48%)
  matrix products  94.5 us (34%)
  starting transfers between devices  18 us (6%)
  local copies, waits for them, and re-layouts  15.2 us (5%)
  waiting for transfers between devices  7.63 us (3%)
  other arithmetic  5.48 us (2%)
    all_to_all x1, blocking collectives, sent_to_all(): return lax.all_to_all(copies, axis, split_axis=0, concat_axis=0, tiled=True)  68 us
    dot_general x4, matrix products, sketch_step(): lax.dot_general(tests, tile_at(index), (((1,), (1,)), ((), ())), precisio...  52.6 us
    psum x5, blocking collectives, over_axes(): array = lax.psum(array, axis)  45.2 us
    dot_general x4, matrix products, image_step(): piece = jnp.dot(basis, tile_at(index), precision=lax.Precision.HIGHEST)  41.3 us
    all_to_all x1, blocking collectives, summed_on_arrival(): lax.all_to_all(parts, axis, split_axis=0, concat_axis=0, tiled=True)  19.5 us
    all_to_all x2, starting transfers between devices, sent_to_all(): return lax.all_to_all(copies, axis, split_axis=0, concat_axis=0, tiled=True)  18 us
    slice x16, local copies, waits for them, and re-layouts, kernel_tile(): first = (rows[0][:, None] - cols[0][None, :]).astype(jnp.float32)  11.2 us
    all_to_all x2, waiting for transfers between devices, sent_to_all(): return lax.all_to_all(copies, axis, split_axis=0, concat_axis=0, tiled=True)  7.63 us
  transfers between devices with their start and end apart: 2, of which 1 were waited for; matrix products, arithmetic and copies ran while one was open for 0% of the time, Pallas kernels for 0%

commit v1 on v0

v1 whole, which is shorter than its diff:
```python
import functools
import math

import jax
import jax.numpy as jnp
from jax import lax
from jax.experimental import pallas as pl
from jax.experimental.pallas import tpu as pltpu
from jax.sharding import Mesh
from jax.sharding import PartitionSpec as P

ROW = ("zl", "y", "c")
COL = ("x", "zh")
RATE = math.log2(math.e) / 6.4
F32 = jnp.float32
BF16 = jnp.bfloat16
HIGHEST = lax.Precision.HIGHEST
LANES = 128
NT = (((1,), (1,)), ((), ()))
TINY = pl.CostEstimate(flops=1, bytes_accessed=1, transcendentals=0)


def exchanged(blocks, axes):
    return lax.all_to_all(blocks, axes, split_axis=0, concat_axis=0, tiled=True)


def features(cells, of_rows):
    v = cells.astype(F32)
    norm = v[0:1] * v[0:1] + v[1:2] * v[1:2] + v[2:3] * v[2:3]
    high = jnp.floor(norm * (1.0 / 128.0)) * 128.0
    low = norm - high
    one = jnp.ones_like(norm)
    if of_rows:
        parts = [-2.0 * v, one, one, high, low, jnp.zeros_like(norm)]
    else:
        parts = [v, high, low, one, one, jnp.zeros_like(norm)]
    return jnp.concatenate(parts, 0)


def in_two(value):
    high = value.astype(BF16)
    return high, (value - high.astype(F32)).astype(BF16)


def sketch_kernel(step_rows, rows_ref, cols_ref, tests_ref, sketch_ref, high_ref, low_ref, total, row_features):
    step = pl.program_id(0)

    @pl.when(step == 0)
    def _():
        row_features[...] = features(rows_ref[...], True).T.astype(BF16)
        total[...] = jnp.zeros_like(total)

    col_features = features(cols_ref[...], False).astype(BF16)
    tests = jnp.concatenate(in_two(tests_ref[...]), 0)
    for start in range(0, total.shape[1], step_rows):
        here = slice(start, start + step_rows)
        squared = jnp.dot(row_features[here, :], col_features, preferred_element_type=F32)
        squared = jnp.maximum(squared, 1e-20)
        high, low = in_two(jnp.exp2((squared * -RATE) * lax.rsqrt(squared)))
        high_ref[here, :] = high
        low_ref[here, :] = low
        total[:, here] += lax.dot_general(
            tests, high, NT, preferred_element_type=F32
        ) + lax.dot_general(tests, low, NT, preferred_element_type=F32)

    @pl.when(step == pl.num_programs(0) - 1)
    def _():
        rank = total.shape[0] // 2
        part = (total[:rank, :] + total[rank:, :]) * 0.25
        quarter = sketch_ref.shape[2]
        for peer in range(sketch_ref.shape[0]):
            sketch_ref[peer] = part[:, peer * quarter : (peer + 1) * quarter]


def sketch_call(row_cells, col_cells, omega, peers, width, step_rows):
    rank, cols = omega.shape
    rows = row_cells.shape[1]
    return pl.pallas_call(
        functools.partial(sketch_kernel, step_rows),
        grid=(cols // width,),
        in_specs=[
            pl.BlockSpec((3, rows), lambda i: (0, 0)),
            pl.BlockSpec((3, width), lambda i: (0, i)),
            pl.BlockSpec((rank, width), lambda i: (0, i)),
        ],
        out_specs=[
            pl.BlockSpec((peers, rank, rows // peers), lambda i: (0, 0, 0)),
            pl.BlockSpec((rows, width), lambda i: (0, i)),
            pl.BlockSpec((rows, width), lambda i: (0, i)),
            pl.BlockSpec((2 * rank, rows), lambda i: (0, 0)),
        ],
        out_shape=[
            jax.ShapeDtypeStruct((peers, rank, rows // peers), F32),
            jax.ShapeDtypeStruct((rows, cols), BF16),
            jax.ShapeDtypeStruct((rows, cols), BF16),
            jax.ShapeDtypeStruct((2 * rank, rows), F32),
        ],
        scratch_shapes=[pltpu.VMEM((rows, 8), BF16)],
        compiler_params=pltpu.CompilerParams(vmem_limit_bytes=62 << 20),
        name="sketch",
    )(row_cells, col_cells, omega)[:3]


def resend_kernel(arrived_ref, sent_ref):
    total = jnp.sum(arrived_ref[...], axis=0)
    for copy in range(sent_ref.shape[0]):
        sent_ref[copy] = total


def resend_call(arrived, copies, name):
    return pl.pallas_call(
        resend_kernel,
        out_shape=jax.ShapeDtypeStruct((copies, *arrived.shape[1:]), F32),
        cost_estimate=TINY,
        name=name,
    )(arrived)


def packed(square):
    half = square.shape[0] // 2
    rest = jnp.zeros((half, LANES - square.shape[1] * 2), F32)
    return jnp.concatenate([square[:half], square[half:], rest], 1)


def unpacked(tile, rank):
    return jnp.concatenate([tile[:, :rank], tile[:, rank : 2 * rank]], 0)


def image_kernel(share, arrived_ref, high_ref, low_ref, parts_ref, sketch_ref, left, gram):
    rank = arrived_ref.shape[1]

    @pl.when(pl.program_id(0) == 0)
    def _():
        sketch = jnp.concatenate([arrived_ref[peer] for peer in range(arrived_ref.shape[0])], 1)
        sketch_ref[...] = sketch
        left[...] = jnp.concatenate(in_two(sketch * 0.25), 0)
        gram[...] = packed(
            lax.dot_general(sketch, sketch, NT, precision=HIGHEST, preferred_element_type=F32)
        )

    product = jnp.dot(left[...], high_ref[...], preferred_element_type=F32) + jnp.dot(
        left[...], low_ref[...], preferred_element_type=F32
    )
    product = product[:rank] + product[rank:]
    pieces = share // LANES
    for block in range(parts_ref.shape[0]):
        for piece in range(pieces):
            at = block * share + piece * LANES
            parts_ref[block, piece * rank : (piece + 1) * rank, :] = product[:, at : at + LANES]
        parts_ref[block, pieces * rank :, :] = gram[...]


def image_call(arrived, high, low, peers, width):
    senders, rank, quarter = arrived.shape
    rows, cols = high.shape
    share = cols // peers
    height = share // LANES * rank + 8
    return pl.pallas_call(
        functools.partial(image_kernel, share),
        grid=(cols // width,),
        in_specs=[
            pl.BlockSpec((senders, rank, quarter), lambda i: (0, 0, 0)),
            pl.BlockSpec((rows, width), lambda i: (0, i)),
            pl.BlockSpec((rows, width), lambda i: (0, i)),
        ],
        out_specs=[
            pl.BlockSpec((width // share, height, LANES), lambda i: (i, 0, 0)),
            pl.BlockSpec((rank, rows), lambda i: (0, 0)),
        ],
        out_shape=[
            jax.ShapeDtypeStruct((peers, height, LANES), F32),
            jax.ShapeDtypeStruct((rank, rows), F32),
        ],
        scratch_shapes=[pltpu.VMEM((2 * rank, rows), BF16), pltpu.VMEM((8, LANES), F32)],
        compiler_params=pltpu.CompilerParams(vmem_limit_bytes=48 << 20),
        name="image",
    )(arrived, high, low)


def inverse_factor(gram):
    rank = gram.shape[0]
    row = lax.broadcasted_iota(jnp.int32, (rank, 1), 0)
    eye = (
        lax.broadcasted_iota(jnp.int32, (rank, rank), 0)
        == lax.broadcasted_iota(jnp.int32, (rank, rank), 1)
    ).astype(F32)
    state = jnp.concatenate([gram, eye, jnp.zeros((rank, LANES - 2 * rank), F32)], 1)
    for k in range(rank):
        scale = lax.rsqrt(state[k : k + 1, k : k + 1])
        pivot = state[k : k + 1, :] * scale
        column = state[:, k : k + 1] * scale
        below = state - column * pivot
        state = jnp.where(row > k, below, jnp.where(row == k, pivot, state))
    return state[:, rank : 2 * rank]


def factor_kernel(rows_total, arrived_ref, sketch_ref, share_ref, basis_ref):
    total = jnp.sum(arrived_ref[...], axis=0)
    rank = sketch_ref.shape[0]
    height = total.shape[0] - 8
    inverse = inverse_factor(unpacked(total[height:], rank) * (1.0 / rows_total))
    for piece in range(0, height, rank):
        part = jnp.dot(
            inverse, total[piece : piece + rank], precision=HIGHEST, preferred_element_type=F32
        )
        for copy in range(share_ref.shape[0]):
            share_ref[copy, piece : piece + rank, :] = part
    basis_ref[...] = jnp.dot(
        inverse, sketch_ref[...], precision=HIGHEST, preferred_element_type=F32
    )


def factor_call(arrived, sketch, rows_total):
    peers, height, _ = arrived.shape
    return pl.pallas_call(
        functools.partial(factor_kernel, rows_total),
        out_shape=[
            jax.ShapeDtypeStruct((peers, height - 8, LANES), F32),
            jax.ShapeDtypeStruct(sketch.shape, F32),
        ],
        name="factor",
    )(arrived, sketch)


def core_kernel(order, arrived_ref, core_ref):
    total = jnp.sum(arrived_ref[...], axis=0)
    core_ref[...] = unpacked(total, core_ref.shape[0]) * (1.0 / order)


def core_call(arrived, rank, order):
    return pl.pallas_call(
        functools.partial(core_kernel, order),
        out_shape=jax.ShapeDtypeStruct((rank, rank), F32),
        cost_estimate=TINY,
        name="core",
    )(arrived)


def joined_kernel(arrived_ref, image_ref, core_ref):
    rank = image_ref.shape[0]
    height = arrived_ref.shape[1]
    at = 0
    for peer in range(arrived_ref.shape[0]):
        for piece in range(0, height, rank):
            image_ref[:, at : at + LANES] = arrived_ref[peer, piece : piece + rank, :]
            at += LANES
    image = image_ref[...]
    tile = packed(
        lax.dot_general(image, image, NT, precision=HIGHEST, preferred_element_type=F32)
    )
    for copy in range(core_ref.shape[0]):
        core_ref[copy] = tile


def joined_call(arrived, rank, copies):
    peers, height, _ = arrived.shape
    return pl.pallas_call(
        joined_kernel,
        out_shape=[
            jax.ShapeDtypeStruct((rank, peers * height // rank * LANES), F32),
            jax.ShapeDtypeStruct((copies, 8, LANES), F32),
        ],
        name="joined",
    )(arrived)


def shards(row_cells, col_cells, omega):
    rank = omega.shape[0]
    local_rows = row_cells.shape[1]
    local_cols = col_cells.shape[1]
    rows_total = local_rows * lax.axis_size(ROW)
    order = local_cols * lax.axis_size(COL)
    peers = lax.axis_size("x")
    parts, high, low = sketch_call(row_cells, col_cells, omega, peers, 1024, 256)
    over_x = resend_call(exchanged(parts, "x"), lax.axis_size("zh"), "over_x")
    over_both = resend_call(exchanged(over_x, "zh"), peers, "over_zh")
    image_parts, sketch = image_call(exchanged(over_both, "x"), high, low, lax.axis_size(ROW), 2048)
    shares, basis = factor_call(exchanged(image_parts, ROW), sketch, rows_total)
    image, core_parts = joined_call(exchanged(shares, ROW), rank, lax.axis_size(COL))
    core = core_call(exchanged(core_parts, COL), rank, order)
    return (basis, image, core)


def solution(mesh):
    finer = Mesh(mesh.devices.reshape(4, 4, 2, 4, 4), ROW + COL)
    return jax.shard_map(
        shards,
        mesh=finer,
        in_specs=(P(None, ROW), P(None, COL), P(None, COL)),
        out_specs=(P(None, ROW), P(None, COL), P()),
        check_vma=False,
    )
```

time: 279 us -> 162 us (0.58); the launches traced: 275 us -> 161 us
  matrix products: 94.5 us -> 0 us
  Pallas kernels: 0 us -> 47.3 us
  blocking collectives: 133 us -> 113 us
  starting transfers between devices: 18 us -> 0 us
  local copies, waits for them, and re-layouts: 15.2 us -> 0.01 us
  waiting for transfers between devices: 7.63 us -> 0 us
  other arithmetic: 5.48 us -> 0 us
    dot_general x10 -> x0, matrix products: 94.2 us -> none  [the longest x4 52.6 us: sketch_step(): lax.dot_general(tests, tile_at(index), (((1,), (1,)), ((), ())), precisio...]
    pallas_call x0 -> x7, Pallas kernels: none -> 47.3 us  [the longest x1 24.1 us: sketch_call(): pl.pallas_call(functools.partial(sketch_kernel, step_rows), grid=(cols //...]
    psum x5 -> x0, blocking collectives: 45.2 us -> none  [over_axes(): array = lax.psum(array, axis)]
    all_to_all x2 -> x6, blocking collectives: 87.6 us -> 113 us  [exchanged(): return lax.all_to_all(blocks, axes, split_axis=0, concat_axis=0, tiled=True)]
    all_to_all x2 -> x0, starting transfers between devices: 18 us -> none  [sent_to_all(): return lax.all_to_all(copies, axis, split_axis=0, concat_axis=0, tiled=True)]
    slice x16 -> x0, local copies, waits for them, and re-layouts: 11.2 us -> none  [kernel_tile(): first = (rows[0][:, None] - cols[0][None, :]).astype(jnp.float32)]
    all_to_all x2 -> x0, waiting for transfers between devices: 7.63 us -> none  [sent_to_all(): return lax.all_to_all(copies, axis, split_axis=0, concat_axis=0, tiled=True)]
    another operation x5 -> x0, other arithmetic: 4.01 us -> none  [the longest x3 2.13 us: shards(): lower = jnp.linalg.cholesky(gram)]
  transfers between devices with their start and end apart: 2 -> 0, of which waited for: 1 -> 0; matrix products, arithmetic and copies ran while one was open for 0% -> 0% of each run, Pallas kernels for 0% -> 0%
where the time goes in v1:
time: 162 us; the launch traced here: 161 us
  blocking collectives  113 us (70%)
  Pallas kernels  47.3 us (29%)
    all_to_all x6, blocking collectives, exchanged(): return lax.all_to_all(blocks, axes, split_axis=0, concat_axis=0, tiled=True)  113 us
    pallas_call x1, Pallas kernels, sketch_call(): pl.pallas_call(functools.partial(sketch_kernel, step_rows), grid=(cols //...  24.1 us
    pallas_call x1, Pallas kernels, image_call(): pl.pallas_call(functools.partial(image_kernel, share), grid=(cols // widt...  12.7 us
    pallas_call x1, Pallas kernels, factor_call(): pl.pallas_call(functools.partial(factor_kernel, rows_total), out_shape=[j...  3.5 us

profile of v1, /device:TPU:1, one launch (start us, length us, event | category | flops | bytes accessed | tf_op | source)
XLA Modules:
  0.0 161.1 jit_solution(5599300824213373861)
XLA Ops:
  0.6 24.1 %sketch.1 = (f32[4,16,256]{2,1,0:T(8,128)}, bf16[1024,8192]{1,0:T(8,128)(2,1)}, bf16[1024,8192]{1,0:T(8,128)(2,1)}, f32[32,1024]{1,0:T(8,128)}) custom-call(s32[3,1024]{1,0:T(4,128)} %rows_ref.1, s32[3,8192]{1,0:T(4,128)} %cols_ref.1, f32[16,8192]{1,0:T(8,128)} %tests_ref.1), custom_call_target="tpu_custom_call" | custom-call | tf_op jit(solution)/shard_map/sketch/pallas_call | solution.py:78
  24.7 9.4 %all_to_all.30.arrived_ref = f32[4,16,256]{2,1,0:T(8,128)} all-to-all(f32[4,16,256]{2,1,0:T(8,128)} %get-tuple-element.12), channel_id=1, replica_groups=mesh['zl'=4,'y'=4,'c'=2,'x'=4,'zh'=4] {'x'}, dimensions={0} | all-to-all | bytes 131072 | tf_op jit(solution)/shard_map/all_to_all | solution.py:24
  34.2 1.5 over_x.1
  35.6 26.8 %all_to_all.31.arrived_ref = f32[4,16,256]{2,1,0:T(8,128)} all-to-all(f32[4,16,256]{2,1,0:T(8,128)} %over_x.1), channel_id=1, replica_groups=mesh['zl'=4,'y'=4,'c'=2,'x'=4,'zh'=4] {'zh'}, dimensions={0} | all-to-all | bytes 131072 | tf_op jit(solution)/shard_map/all_to_all | solution.py:24
  62.4 1.5 over_zh.1
  63.9 7.7 %all_to_all.32.arrived_ref = f32[4,16,256]{2,1,0:T(8,128)S(1)} all-to-all(f32[4,16,256]{2,1,0:T(8,128)} %over_zh.1), channel_id=1, replica_groups=mesh['zl'=4,'y'=4,'c'=2,'x'=4,'zh'=4] {'x'}, dimensions={0} | all-to-all | bytes 131072 | tf_op jit(solution)/shard_map/all_to_all | solution.py:24
  71.6 12.7 %image.1 = (f32[32,40,128]{2,1,0:T(8,128)S(1)}, f32[16,1024]{1,0:T(8,128)S(1)}) custom-call(f32[4,16,256]{2,1,0:T(8,128)S(1)} %all_to_all.32.arrived_ref, bf16[1024,8192]{1,0:T(8,128)(2,1)} %get-tuple-element.13.high_ref, bf16[1024,8192]{1,0:T(8,128)(2,1)} %get-tuple-element.14.low_ref), custom_call_target="tpu_custom_call" | custom-call | tf_op jit(solution)/shard_map/image/pallas_call | solution.py:158
  84.3 0.0 copy-start
  84.3 29.5 %all_to_all.33.arrived_ref = f32[32,40,128]{2,1,0:T(8,128)} all-to-all(f32[32,40,128]{2,1,0:T(8,128)S(1)} %get-tuple-element.15), channel_id=1, replica_groups=mesh['zl'=4,'y'=4,'c'=2,'x'=4,'zh'=4] {'zl','y','c'}, dimensions={0} | all-to-all | bytes 1310720 | tf_op jit(solution)/shard_map/all_to_all | solution.py:24
  113.8 0.0 copy-done
  113.8 3.5 %factor.1 = (f32[32,32,128]{2,1,0:T(8,128)}, f32[16,1024]{1,0:T(8,128)}) custom-call(f32[32,40,128]{2,1,0:T(8,128)} %all_to_all.33.arrived_ref, f32[16,1024]{1,0:T(8,128)} %copy-done), custom_call_target="tpu_custom_call" | custom-call | tf_op jit(solution)/shard_map/factor/pallas_call | solution.py:215
  117.3 20.9 %all_to_all.34.arrived_ref = f32[32,32,128]{2,1,0:T(8,128)} all-to-all(f32[32,32,128]{2,1,0:T(8,128)} %get-tuple-element.18), channel_id=1, replica_groups=mesh['zl'=4,'y'=4,'c'=2,'x'=4,'zh'=4] {'zl','y','c'}, dimensions={0} | all-to-all | bytes 1048576 | tf_op jit(solution)/shard_map/all_to_all | solution.py:24
  138.2 2.6 %joined.1 = (f32[16,8192]{1,0:T(8,128)}, f32[16,8,128]{2,1,0:T(8,128)}) custom-call(f32[32,32,128]{2,1,0:T(8,128)} %all_to_all.34.arrived_ref), custom_call_target="tpu_custom_call" | custom-call | tf_op jit(solution)/shard_map/joined/pallas_call | solution.py:257
  140.8 18.8 %all_to_all.35.arrived_ref = f32[16,8,128]{2,1,0:T(8,128)} all-to-all(f32[16,8,128]{2,1,0:T(8,128)} %get-tuple-element.20), channel_id=1, replica_groups=mesh['zl'=4,'y'=4,'c'=2,'x'=4,'zh'=4] {'x','zh'}, dimensions={0} | all-to-all | bytes 131072 | tf_op jit(solution)/shard_map/all_to_all | solution.py:24
  159.6 1.5 core.1
Async XLA Ops:
  84.3 29.5 %copy-start = (f32[16,1024]{1,0:T(8,128)}, f32[16,1024]{1,0:T(8,128)S(1)}, u32[]{:S(2)}) copy-start(f32[16,1024]{1,0:T(8,128)S(1)} %get-tuple-element.16.sketch_ref) | copy-start | bytes 196612

commit v2 on v1

--- a/solution.py
+++ b/solution.py
@@ -17,7 +17,8 @@
 HIGHEST = lax.Precision.HIGHEST
 LANES = 128
 NT = (((1,), (1,)), ((), ()))
-TINY = pl.CostEstimate(flops=1, bytes_accessed=1, transcendentals=0)
+VMEM = pl.BlockSpec(memory_space=pltpu.VMEM)
+SMALL = pltpu.CompilerParams(vmem_limit_bytes=8 << 20)
 
 
 def exchanged(blocks, axes):
@@ -42,7 +43,7 @@
     return high, (value - high.astype(F32)).astype(BF16)
 
 
-def sketch_kernel(step_rows, rows_ref, cols_ref, tests_ref, sketch_ref, high_ref, low_ref, total, row_features):
+def sketch_kernel(rows_ref, cols_ref, tests_ref, sketch_ref, matrix_ref, total, row_features):
     step = pl.program_id(0)
 
     @pl.when(step == 0)
@@ -52,16 +53,28 @@
 
     col_features = features(cols_ref[...], False).astype(BF16)
     tests = jnp.concatenate(in_two(tests_ref[...]), 0)
-    for start in range(0, total.shape[1], step_rows):
-        here = slice(start, start + step_rows)
-        squared = jnp.dot(row_features[here, :], col_features, preferred_element_type=F32)
+    blocks, _, _, width = matrix_ref.shape
+
+    def evaluated(block):
+        here = slice(block * width, (block + 1) * width)
+        squared = jnp.dot(row_features[...], col_features[:, here], preferred_element_type=F32)
         squared = jnp.maximum(squared, 1e-20)
         high, low = in_two(jnp.exp2((squared * -RATE) * lax.rsqrt(squared)))
-        high_ref[here, :] = high
-        low_ref[here, :] = low
-        total[:, here] += lax.dot_general(
-            tests, high, NT, preferred_element_type=F32
-        ) + lax.dot_general(tests, low, NT, preferred_element_type=F32)
+        matrix_ref[block, 0] = high
+        matrix_ref[block, 1] = low
+        return tests[:, here], high, low
+
+    def summed(left, high, low):
+        total[...] += lax.dot_general(
+            left, high, NT, preferred_element_type=F32
+        ) + lax.dot_general(left, low, NT, preferred_element_type=F32)
+
+    waiting = evaluated(0)
+    for block in range(1, blocks):
+        latest = evaluated(block)
+        summed(*waiting)
+        waiting = latest
+    summed(*waiting)
 
     @pl.when(step == pl.num_programs(0) - 1)
     def _():
@@ -72,33 +85,32 @@
             sketch_ref[peer] = part[:, peer * quarter : (peer + 1) * quarter]
 
 
-def sketch_call(row_cells, col_cells, omega, peers, width, step_rows):
+def sketch_call(row_cells, col_cells, omega, peers, blocks, together):
     rank, cols = omega.shape
     rows = row_cells.shape[1]
-    return pl.pallas_call(
-        functools.partial(sketch_kernel, step_rows),
-        grid=(cols // width,),
+    width = cols // blocks
+    return pl.pallas_call(
+        sketch_kernel,
+        grid=(blocks // together,),
         in_specs=[
             pl.BlockSpec((3, rows), lambda i: (0, 0)),
-            pl.BlockSpec((3, width), lambda i: (0, i)),
-            pl.BlockSpec((rank, width), lambda i: (0, i)),
+            pl.BlockSpec((3, together * width), lambda i: (0, i)),
+            pl.BlockSpec((rank, together * width), lambda i: (0, i)),
         ],
         out_specs=[
             pl.BlockSpec((peers, rank, rows // peers), lambda i: (0, 0, 0)),
-            pl.BlockSpec((rows, width), lambda i: (0, i)),
-            pl.BlockSpec((rows, width), lambda i: (0, i)),
+            pl.BlockSpec((together, 2, rows, width), lambda i: (i, 0, 0, 0)),
             pl.BlockSpec((2 * rank, rows), lambda i: (0, 0)),
         ],
         out_shape=[
             jax.ShapeDtypeStruct((peers, rank, rows // peers), F32),
-            jax.ShapeDtypeStruct((rows, cols), BF16),
-            jax.ShapeDtypeStruct((rows, cols), BF16),
+            jax.ShapeDtypeStruct((blocks, 2, rows, width), BF16),
             jax.ShapeDtypeStruct((2 * rank, rows), F32),
         ],
         scratch_shapes=[pltpu.VMEM((rows, 8), BF16)],
         compiler_params=pltpu.CompilerParams(vmem_limit_bytes=62 << 20),
         name="sketch",
-    )(row_cells, col_cells, omega)[:3]
+    )(row_cells, col_cells, omega)[:2]
 
 
 def resend_kernel(arrived_ref, sent_ref):
@@ -110,8 +122,10 @@
 def resend_call(arrived, copies, name):
     return pl.pallas_call(
         resend_kernel,
+        in_specs=[VMEM],
+        out_specs=VMEM,
         out_shape=jax.ShapeDtypeStruct((copies, *arrived.shape[1:]), F32),
-        cost_estimate=TINY,
+        compiler_params=SMALL,
         name=name,
     )(arrived)
 
@@ -126,55 +140,62 @@
     return jnp.concatenate([tile[:, :rank], tile[:, rank : 2 * rank]], 0)
 
 
-def image_kernel(share, arrived_ref, high_ref, low_ref, parts_ref, sketch_ref, left, gram):
-    rank = arrived_ref.shape[1]
-
-    @pl.when(pl.program_id(0) == 0)
-    def _():
-        sketch = jnp.concatenate([arrived_ref[peer] for peer in range(arrived_ref.shape[0])], 1)
-        sketch_ref[...] = sketch
-        left[...] = jnp.concatenate(in_two(sketch * 0.25), 0)
-        gram[...] = packed(
-            lax.dot_general(sketch, sketch, NT, precision=HIGHEST, preferred_element_type=F32)
+def image_kernel(together, arrived_ref, matrix_hbm, parts_ref, sketch_ref, matrix, arrivals):
+    blocks, _, _, width = matrix.shape
+
+    def copy_of(block):
+        return pltpu.make_async_copy(
+            matrix_hbm.at[block], matrix.at[block], arrivals.at[block]
         )
 
-    product = jnp.dot(left[...], high_ref[...], preferred_element_type=F32) + jnp.dot(
-        left[...], low_ref[...], preferred_element_type=F32
+    for block in range(blocks):
+        copy_of(block).start()
+    senders, rank, _ = arrived_ref.shape
+    sketch = jnp.concatenate([arrived_ref[peer] for peer in range(senders)], 1)
+    sketch_ref[...] = sketch
+    left = jnp.concatenate(in_two(sketch * 0.25), 0)
+    gram = packed(
+        lax.dot_general(sketch, sketch, NT, precision=HIGHEST, preferred_element_type=F32)
     )
-    product = product[:rank] + product[rank:]
-    pieces = share // LANES
-    for block in range(parts_ref.shape[0]):
-        for piece in range(pieces):
-            at = block * share + piece * LANES
-            parts_ref[block, piece * rank : (piece + 1) * rank, :] = product[:, at : at + LANES]
-        parts_ref[block, pieces * rank :, :] = gram[...]
-
-
-def image_call(arrived, high, low, peers, width):
+
+    def step(index, carry):
+        for offset in range(together):
+            copy_of(index * together + offset).wait()
+        for offset in range(together):
+            block = index * together + offset
+            product = jnp.dot(
+                left, matrix[block, 0], preferred_element_type=F32
+            ) + jnp.dot(left, matrix[block, 1], preferred_element_type=F32)
+            product = product[:rank] + product[rank:]
+            for piece in range(width // LANES):
+                parts_ref[block, piece * rank : (piece + 1) * rank, :] = product[
+                    :, piece * LANES : (piece + 1) * LANES
+                ]
+            parts_ref[block, width // LANES * rank :, :] = gram
+        return carry
+
+    lax.fori_loop(0, blocks // together, step, 0)
+
+
+def image_call(arrived, matrix, together):
     senders, rank, quarter = arrived.shape
-    rows, cols = high.shape
-    share = cols // peers
-    height = share // LANES * rank + 8
-    return pl.pallas_call(
-        functools.partial(image_kernel, share),
-        grid=(cols // width,),
-        in_specs=[
-            pl.BlockSpec((senders, rank, quarter), lambda i: (0, 0, 0)),
-            pl.BlockSpec((rows, width), lambda i: (0, i)),
-            pl.BlockSpec((rows, width), lambda i: (0, i)),
-        ],
-        out_specs=[
-            pl.BlockSpec((width // share, height, LANES), lambda i: (i, 0, 0)),
-            pl.BlockSpec((rank, rows), lambda i: (0, 0)),
-        ],
+    blocks, _, rows, width = matrix.shape
+    height = width // LANES * rank + 8
+    return pl.pallas_call(
+        functools.partial(image_kernel, together),
+        in_specs=[VMEM, pl.BlockSpec(memory_space=pl.ANY)],
+        out_specs=[VMEM, VMEM],
         out_shape=[
-            jax.ShapeDtypeStruct((peers, height, LANES), F32),
+            jax.ShapeDtypeStruct((blocks, height, LANES), F32),
             jax.ShapeDtypeStruct((rank, rows), F32),
         ],
-        scratch_shapes=[pltpu.VMEM((2 * rank, rows), BF16), pltpu.VMEM((8, LANES), F32)],
+        scratch_shapes=[
+            pltpu.VMEM(matrix.shape, BF16),
+            pltpu.SemaphoreType.DMA((blocks,)),
+        ],
         compiler_params=pltpu.CompilerParams(vmem_limit_bytes=48 << 20),
         name="image",
-    )(arrived, high, low)
+    )(arrived, matrix)
 
 
 def inverse_factor(gram):
@@ -214,10 +235,13 @@
     peers, height, _ = arrived.shape
     return pl.pallas_call(
         functools.partial(factor_kernel, rows_total),
+        in_specs=[VMEM, VMEM],
+        out_specs=[VMEM, VMEM],
         out_shape=[
             jax.ShapeDtypeStruct((peers, height - 8, LANES), F32),
             jax.ShapeDtypeStruct(sketch.shape, F32),
         ],
+        compiler_params=SMALL,
         name="factor",
     )(arrived, sketch)
 
@@ -230,8 +254,10 @@
 def core_call(arrived, rank, order):
     return pl.pallas_call(
         functools.partial(core_kernel, order),
+        in_specs=[VMEM],
+        out_specs=VMEM,
         out_shape=jax.ShapeDtypeStruct((rank, rank), F32),
-        cost_estimate=TINY,
+        compiler_params=SMALL,
         name="core",
     )(arrived)
 
@@ -256,10 +282,13 @@
     peers, height, _ = arrived.shape
     return pl.pallas_call(
         joined_kernel,
+        in_specs=[VMEM],
+        out_specs=[VMEM, VMEM],
         out_shape=[
             jax.ShapeDtypeStruct((rank, peers * height // rank * LANES), F32),
             jax.ShapeDtypeStruct((copies, 8, LANES), F32),
         ],
+        compiler_params=SMALL,
         name="joined",
     )(arrived)
 
@@ -271,10 +300,10 @@
     rows_total = local_rows * lax.axis_size(ROW)
     order = local_cols * lax.axis_size(COL)
     peers = lax.axis_size("x")
-    parts, high, low = sketch_call(row_cells, col_cells, omega, peers, 1024, 256)
+    parts, matrix = sketch_call(row_cells, col_cells, omega, peers, lax.axis_size(ROW), 4)
     over_x = resend_call(exchanged(parts, "x"), lax.axis_size("zh"), "over_x")
     over_both = resend_call(exchanged(over_x, "zh"), peers, "over_zh")
-    image_parts, sketch = image_call(exchanged(over_both, "x"), high, low, lax.axis_size(ROW), 2048)
+    image_parts, sketch = image_call(exchanged(over_both, "x"), matrix, 2)
     shares, basis = factor_call(exchanged(image_parts, ROW), sketch, rows_total)
     image, core_parts = joined_call(exchanged(shares, ROW), rank, lax.axis_size(COL))
     core = core_call(exchanged(core_parts, COL), rank, order)

time: 162 us -> 145 us (0.90)
  Pallas kernels: 47.3 us -> 34.6 us
  blocking collectives: 113 us -> 110 us
    pallas_call x7, Pallas kernels: 47.3 us -> 34.6 us  [the longest x1 19 us: sketch_call(): pl.pallas_call(sketch_kernel, grid=(blocks // together,), in_specs=[pl.Bl...]
    all_to_all x6, blocking collectives: 113 us -> 110 us  [exchanged(): return lax.all_to_all(blocks, axes, split_axis=0, concat_axis=0, tiled=True)]
where the time goes in v2:
time: 145 us
  blocking collectives  110 us (76%)
  Pallas kernels  34.6 us (24%)
    all_to_all x6, blocking collectives, exchanged(): return lax.all_to_all(blocks, axes, split_axis=0, concat_axis=0, tiled=True)  110 us
    pallas_call x1, Pallas kernels, sketch_call(): pl.pallas_call(sketch_kernel, grid=(blocks // together,), in_specs=[pl.Bl...  19 us
    pallas_call x1, Pallas kernels, image_call(): pl.pallas_call(functools.partial(image_kernel, together), in_specs=[VMEM,...  11.3 us

profile of v2, /device:TPU:1, one launch (start us, length us, event | category | flops | bytes accessed | tf_op | source)
XLA Modules:
  0.0 144.8 jit_solution(10059573251054381988)
XLA Ops:
  0.6 19.0 %sketch.1 = (f32[4,16,256]{2,1,0:T(8,128)}, bf16[32,2,1024,256]{3,2,1,0:T(8,128)(2,1)}, f32[32,1024]{1,0:T(8,128)}) custom-call(s32[3,1024]{1,0:T(4,128)} %rows_ref.1, s32[3,8192]{1,0:T(4,128)} %cols_ref.1, f32[16,8192]{1,0:T(8,128)} %tests_ref.1), custom_call_target="tpu_custom_call" | custom-call | tf_op jit(solution)/shard_map/sketch/pallas_call | solution.py:92
  19.6 9.3 %all_to_all.30.arrived_ref = f32[4,16,256]{2,1,0:T(8,128)S(1)} all-to-all(f32[4,16,256]{2,1,0:T(8,128)} %get-tuple-element.11), channel_id=1, replica_groups=mesh['zl'=4,'y'=4,'c'=2,'x'=4,'zh'=4] {'x'}, dimensions={0} | all-to-all | bytes 131072 | tf_op jit(solution)/shard_map/all_to_all | solution.py:25
  28.9 26.5 %all_to_all.31.arrived_ref = f32[4,16,256]{2,1,0:T(8,128)S(1)} all-to-all(f32[4,16,256]{2,1,0:T(8,128)S(1)} %over_x.1), channel_id=1, replica_groups=mesh['zl'=4,'y'=4,'c'=2,'x'=4,'zh'=4] {'zh'}, dimensions={0} | all-to-all | bytes 131072 | tf_op jit(solution)/shard_map/all_to_all | solution.py:25
  55.4 6.8 %all_to_all.32.arrived_ref = f32[4,16,256]{2,1,0:T(8,128)S(1)} all-to-all(f32[4,16,256]{2,1,0:T(8,128)S(1)} %over_zh.1), channel_id=1, replica_groups=mesh['zl'=4,'y'=4,'c'=2,'x'=4,'zh'=4] {'x'}, dimensions={0} | all-to-all | bytes 131072 | tf_op jit(solution)/shard_map/all_to_all | solution.py:25
  62.3 11.3 %image.1 = (f32[32,40,128]{2,1,0:T(8,128)S(1)}, f32[16,1024]{1,0:T(8,128)S(1)}) custom-call(f32[4,16,256]{2,1,0:T(8,128)S(1)} %all_to_all.32.arrived_ref, bf16[32,2,1024,256]{3,2,1,0:T(8,128)(2,1)} %get-tuple-element.12.matrix_hbm), custom_call_target="tpu_custom_call" | custom-call | tf_op jit(solution)/shard_map/image/pallas_call | solution.py:184
  73.6 29.4 %all_to_all.33.arrived_ref = f32[32,40,128]{2,1,0:T(8,128)S(1)} all-to-all(f32[32,40,128]{2,1,0:T(8,128)S(1)} %get-tuple-element.13), channel_id=1, replica_groups=mesh['zl'=4,'y'=4,'c'=2,'x'=4,'zh'=4] {'zl','y','c'}, dimensions={0} | all-to-all | bytes 1310720 | tf_op jit(solution)/shard_map/all_to_all | solution.py:25
  103.0 2.3 %factor.1 = (f32[32,32,128]{2,1,0:T(8,128)S(1)}, f32[16,1024]{1,0:T(8,128)}) custom-call(f32[32,40,128]{2,1,0:T(8,128)S(1)} %all_to_all.33.arrived_ref, f32[16,1024]{1,0:T(8,128)S(1)} %get-tuple-element.14.sketch_ref), custom_call_target="tpu_custom_call" | custom-call | tf_op jit(solution)/shard_map/factor/pallas_call | solution.py:236
  105.3 20.6 %all_to_all.34.arrived_ref = f32[32,32,128]{2,1,0:T(8,128)S(1)} all-to-all(f32[32,32,128]{2,1,0:T(8,128)S(1)} %get-tuple-element.16), channel_id=1, replica_groups=mesh['zl'=4,'y'=4,'c'=2,'x'=4,'zh'=4] {'zl','y','c'}, dimensions={0} | all-to-all | bytes 1048576 | tf_op jit(solution)/shard_map/all_to_all | solution.py:25
  125.9 1.4 joined.1
  127.2 16.9 %all_to_all.35.arrived_ref = f32[16,8,128]{2,1,0:T(8,128)S(1)} all-to-all(f32[16,8,128]{2,1,0:T(8,128)S(1)} %get-tuple-element.18), channel_id=1, replica_groups=mesh['zl'=4,'y'=4,'c'=2,'x'=4,'zh'=4] {'x','zh'}, dimensions={0} | all-to-all | bytes 131072 | tf_op jit(solution)/shard_map/all_to_all | solution.py:25
  144.2 0.7 core.1
  (2 shorter events, 0.0 us)

commit v3 on v2

--- a/solution.py
+++ b/solution.py
@@ -23,6 +23,10 @@
 
 def exchanged(blocks, axes):
     return lax.all_to_all(blocks, axes, split_axis=0, concat_axis=0, tiled=True)
+
+
+def swapped(block):
+    return lax.ppermute(block, "c", [(0, 1), (1, 0)])
 
 
 def features(cells, of_rows):
@@ -140,23 +144,14 @@
     return jnp.concatenate([tile[:, :rank], tile[:, rank : 2 * rank]], 0)
 
 
-def image_kernel(together, arrived_ref, matrix_hbm, parts_ref, sketch_ref, matrix, arrivals):
+def image_blocks(together, core, left, gram, matrix_hbm, parts_ref, matrix, arrivals):
     blocks, _, _, width = matrix.shape
+    rank = left.shape[0] // 2
 
     def copy_of(block):
         return pltpu.make_async_copy(
-            matrix_hbm.at[block], matrix.at[block], arrivals.at[block]
+            matrix_hbm.at[2 * block + core], matrix.at[block], arrivals.at[block]
         )
-
-    for block in range(blocks):
-        copy_of(block).start()
-    senders, rank, _ = arrived_ref.shape
-    sketch = jnp.concatenate([arrived_ref[peer] for peer in range(senders)], 1)
-    sketch_ref[...] = sketch
-    left = jnp.concatenate(in_two(sketch * 0.25), 0)
-    gram = packed(
-        lax.dot_general(sketch, sketch, NT, precision=HIGHEST, preferred_element_type=F32)
-    )
 
     def step(index, carry):
         for offset in range(together):
@@ -164,38 +159,101 @@
         for offset in range(together):
             block = index * together + offset
             product = jnp.dot(
-                left, matrix[block, 0], preferred_element_type=F32
-            ) + jnp.dot(left, matrix[block, 1], preferred_element_type=F32)
+                left[...], matrix[block, 0], preferred_element_type=F32
+            ) + jnp.dot(left[...], matrix[block, 1], preferred_element_type=F32)
             product = product[:rank] + product[rank:]
             for piece in range(width // LANES):
                 parts_ref[block, piece * rank : (piece + 1) * rank, :] = product[
                     :, piece * LANES : (piece + 1) * LANES
                 ]
-            parts_ref[block, width // LANES * rank :, :] = gram
+            parts_ref[block, width // LANES * rank :, :] = gram[...]
         return carry
 
+    for block in range(blocks):
+        copy_of(block).start()
+    yield
     lax.fori_loop(0, blocks // together, step, 0)
 
 
-def image_call(arrived, matrix, together):
+def first_kernel(
+    together, arrived_ref, matrix_hbm, parts_ref, sketch_ref, left_ref, gram_ref, matrix, arrivals
+):
+    core = 1 - lax.axis_index("c")
+    work = image_blocks(
+        together, core, left_ref, gram_ref, matrix_hbm, parts_ref, matrix, arrivals
+    )
+    next(work)
+    senders = arrived_ref.shape[0]
+    sketch = jnp.concatenate([arrived_ref[peer] for peer in range(senders)], 1)
+    sketch_ref[...] = sketch
+    left_ref[...] = jnp.concatenate(in_two(sketch * 0.25), 0)
+    gram_ref[...] = packed(
+        lax.dot_general(sketch, sketch, NT, precision=HIGHEST, preferred_element_type=F32)
+    )
+    for _ in work:
+        pass
+
+
+def second_kernel(together, left_ref, gram_ref, matrix_hbm, parts_ref, matrix, arrivals):
+    core = lax.axis_index("c")
+    for _ in image_blocks(
+        together, core, left_ref, gram_ref, matrix_hbm, parts_ref, matrix, arrivals
+    ):
+        pass
+
+
+def image_calls(arrived, matrix, together):
     senders, rank, quarter = arrived.shape
     blocks, _, rows, width = matrix.shape
-    height = width // LANES * rank + 8
-    return pl.pallas_call(
-        functools.partial(image_kernel, together),
+    half = blocks // 2
+    parts = jax.ShapeDtypeStruct((half, width // LANES * rank + 8, LANES), F32)
+    options = {
+        "scratch_shapes": [
+            pltpu.VMEM((half, *matrix.shape[1:]), BF16),
+            pltpu.SemaphoreType.DMA((half,)),
+        ],
+        "compiler_params": pltpu.CompilerParams(vmem_limit_bytes=32 << 20),
+        "cost_estimate": pl.CostEstimate(
+            flops=4 * rank * matrix.size, bytes_accessed=matrix.size, transcendentals=0
+        ),
+    }
+    first, sketch, left, gram = pl.pallas_call(
+        functools.partial(first_kernel, together),
         in_specs=[VMEM, pl.BlockSpec(memory_space=pl.ANY)],
-        out_specs=[VMEM, VMEM],
+        out_specs=[VMEM] * 4,
         out_shape=[
-            jax.ShapeDtypeStruct((blocks, height, LANES), F32),
+            parts,
             jax.ShapeDtypeStruct((rank, rows), F32),
-        ],
-        scratch_shapes=[
-            pltpu.VMEM(matrix.shape, BF16),
-            pltpu.SemaphoreType.DMA((blocks,)),
-        ],
-        compiler_params=pltpu.CompilerParams(vmem_limit_bytes=48 << 20),
-        name="image",
+            jax.ShapeDtypeStruct((2 * rank, rows), BF16),
+            jax.ShapeDtypeStruct((8, LANES), F32),
+        ],
+        name="image_of_other",
+        **options,
     )(arrived, matrix)
+    second = pl.pallas_call(
+        functools.partial(second_kernel, together),
+        in_specs=[VMEM, VMEM, pl.BlockSpec(memory_space=pl.ANY)],
+        out_specs=VMEM,
+        out_shape=parts,
+        name="image_of_own",
+        **options,
+    )(left, gram, matrix)
+    return first, second, sketch
+
+
+def pair_kernel(own_ref, other_ref, sum_ref):
+    sum_ref[...] = own_ref[...] + other_ref[...]
+
+
+def pair_call(own, other):
+    return pl.pallas_call(
+        pair_kernel,
+        in_specs=[VMEM, VMEM],
+        out_specs=VMEM,
+        out_shape=jax.ShapeDtypeStruct(own.shape, F32),
+        compiler_params=SMALL,
+        name="pair",
+    )(own, other)
 
 
 def inverse_factor(gram):
@@ -262,35 +320,55 @@
     )(arrived)
 
 
-def joined_kernel(arrived_ref, image_ref, core_ref):
-    rank = image_ref.shape[0]
-    height = arrived_ref.shape[1]
-    at = 0
-    for peer in range(arrived_ref.shape[0]):
-        for piece in range(0, height, rank):
-            image_ref[:, at : at + LANES] = arrived_ref[peer, piece : piece + rank, :]
-            at += LANES
-    image = image_ref[...]
+def square_kernel(arrived_ref, square_ref):
+    senders, height, _ = arrived_ref.shape
+    rank = height // 2
+    pieces = [
+        arrived_ref[sender, piece * rank : (piece + 1) * rank, :]
+        for sender in range(senders)
+        for piece in range(2)
+    ]
+    image = jnp.concatenate(pieces, 1)
     tile = packed(
         lax.dot_general(image, image, NT, precision=HIGHEST, preferred_element_type=F32)
     )
-    for copy in range(core_ref.shape[0]):
-        core_ref[copy] = tile
-
-
-def joined_call(arrived, rank, copies):
-    peers, height, _ = arrived.shape
+    for copy in range(square_ref.shape[0]):
+        square_ref[copy] = tile
+
+
+def square_call(arrived, copies):
+    return pl.pallas_call(
+        square_kernel,
+        in_specs=[VMEM],
+        out_specs=VMEM,
+        out_shape=jax.ShapeDtypeStruct((copies, 8, LANES), F32),
+        compiler_params=SMALL,
+        name="square",
+    )(arrived)
+
+
+def joined_kernel(own_ref, other_ref, image_ref):
+    core = lax.axis_index("c")
+    rank = image_ref.shape[0]
+    senders, height, _ = own_ref.shape
+    pieces = height // rank
+    for sender in range(senders):
+        for ref, half in ((own_ref, core), (other_ref, 1 - core)):
+            for piece in range(pieces):
+                at = pl.multiple_of(((2 * sender + half) * pieces + piece) * LANES, LANES)
+                image_ref[:, pl.ds(at, LANES)] = ref[sender, piece * rank : (piece + 1) * rank, :]
+
+
+def joined_call(own, other, rank):
+    senders, height, _ = own.shape
     return pl.pallas_call(
         joined_kernel,
-        in_specs=[VMEM],
-        out_specs=[VMEM, VMEM],
-        out_shape=[
-            jax.ShapeDtypeStruct((rank, peers * height // rank * LANES), F32),
-            jax.ShapeDtypeStruct((copies, 8, LANES), F32),
-        ],
+        in_specs=[VMEM, VMEM],
+        out_specs=VMEM,
+        out_shape=jax.ShapeDtypeStruct((rank, 2 * senders * height // rank * LANES), F32),
         compiler_params=SMALL,
         name="joined",
-    )(arrived)
+    )(own, other)
 
 
 def shards(row_cells, col_cells, omega):
@@ -303,10 +381,14 @@
     parts, matrix = sketch_call(row_cells, col_cells, omega, peers, lax.axis_size(ROW), 4)
     over_x = resend_call(exchanged(parts, "x"), lax.axis_size("zh"), "over_x")
     over_both = resend_call(exchanged(over_x, "zh"), peers, "over_zh")
-    image_parts, sketch = image_call(exchanged(over_both, "x"), matrix, 2)
-    shares, basis = factor_call(exchanged(image_parts, ROW), sketch, rows_total)
-    image, core_parts = joined_call(exchanged(shares, ROW), rank, lax.axis_size(COL))
-    core = core_call(exchanged(core_parts, COL), rank, order)
+    first, second, sketch = image_calls(exchanged(over_both, "x"), matrix, 2)
+    chip_parts = pair_call(second, swapped(first))
+    shares, basis = factor_call(exchanged(chip_parts, ("zl", "y")), sketch, rows_total)
+    own = exchanged(shares, ("zl", "y"))
+    other = swapped(own)
+    square_parts = square_call(own, lax.axis_size(COL + ("c",)))
+    core = core_call(exchanged(square_parts, COL + ("c",)), rank, order)
+    image = joined_call(own, other, rank)
     return (basis, image, core)
 
 

time: 145 us -> 139 us (0.959)
  blocking collectives: 110 us -> 72.6 us
  starting transfers between devices: 0 us -> 14.8 us
  waiting for transfers between devices: 0 us -> 13.4 us
  Pallas kernels: 34.6 us -> 36.8 us
    all_to_all x6 -> x5, blocking collectives: 110 us -> 72.6 us  [exchanged(): return lax.all_to_all(blocks, axes, split_axis=0, concat_axis=0, tiled=True)]
    all_to_all x0 -> x1, waiting for transfers between devices: none -> 12.3 us  [exchanged(): return lax.all_to_all(blocks, axes, split_axis=0, concat_axis=0, tiled=True)]
    ppermute x0 -> x2, starting transfers between devices: none -> 8.85 us  [swapped(): return lax.ppermute(block, 'c', [(0, 1), (1, 0)])]
    all_to_all x0 -> x1, starting transfers between devices: none -> 5.94 us  [exchanged(): return lax.all_to_all(blocks, axes, split_axis=0, concat_axis=0, tiled=True)]
    pallas_call x2 -> x5, Pallas kernels: 12.7 us -> 14.8 us  [the longest x1 6.4 us: image_calls(): pl.pallas_call(functools.partial(first_kernel, together), in_specs=[VMEM,...]
  transfers between devices with their start and end apart: 0 -> 3, of which waited for: 0 -> 2; matrix products, arithmetic and copies ran while one was open for 0% -> 0% of each run, Pallas kernels for 0% -> 5%
where the time goes in v3:
time: 139 us; the launch traced here: 138 us
  blocking collectives  72.6 us (52%)
  Pallas kernels  36.8 us (26%)
  starting transfers between devices  14.8 us (11%)
  waiting for transfers between devices  13.4 us (10%)
    all_to_all x5, blocking collectives, exchanged(): return lax.all_to_all(blocks, axes, split_axis=0, concat_axis=0, tiled=True)  72.6 us
    pallas_call x1, Pallas kernels, sketch_call(): pl.pallas_call(sketch_kernel, grid=(blocks // together,), in_specs=[pl.Bl...  19 us
    all_to_all x1, waiting for transfers between devices, exchanged(): return lax.all_to_all(blocks, axes, split_axis=0, concat_axis=0, tiled=True)  12.3 us
    ppermute x2, starting transfers between devices, swapped(): return lax.ppermute(block, 'c', [(0, 1), (1, 0)])  8.85 us
    pallas_call x1, Pallas kernels, image_calls(): pl.pallas_call(functools.partial(first_kernel, together), in_specs=[VMEM,...  6.4 us
    pallas_call x1, Pallas kernels, image_calls(): pl.pallas_call(functools.partial(second_kernel, together), in_specs=[VMEM...  6.39 us
    all_to_all x1, starting transfers between devices, exchanged(): return lax.all_to_all(blocks, axes, split_axis=0, concat_axis=0, tiled=True)  5.94 us
  transfers between devices with their start and end apart: 3, of which 2 were waited for; matrix products, arithmetic and copies ran while one was open for 0% of the time, Pallas kernels for 5%

profile of v3, /device:TPU:1, one launch (start us, length us, event | category | flops | bytes accessed | tf_op | source)
XLA Modules:
  0.0 138.4 jit_solution(3526525935122471742)
XLA Ops:
  0.6 19.0 %sketch.1 = (f32[4,16,256]{2,1,0:T(8,128)}, bf16[32,2,1024,256]{3,2,1,0:T(8,128)(2,1)}, f32[32,1024]{1,0:T(8,128)}) custom-call(s32[3,1024]{1,0:T(4,128)} %rows_ref.1, s32[3,8192]{1,0:T(4,128)} %cols_ref.1, f32[16,8192]{1,0:T(8,128)} %tests_ref.1), custom_call_target="tpu_custom_call" | custom-call | tf_op jit(solution)/shard_map/sketch/pallas_call | solution.py:96
  19.6 9.3 %all_to_all.30.arrived_ref = f32[4,16,256]{2,1,0:T(8,128)S(1)} all-to-all(f32[4,16,256]{2,1,0:T(8,128)} %get-tuple-element.11), channel_id=1, replica_groups=mesh['zl'=4,'y'=4,'c'=2,'x'=4,'zh'=4] {'x'}, dimensions={0} | all-to-all | bytes 131072 | tf_op jit(solution)/shard_map/all_to_all | solution.py:25
  28.9 26.5 %all_to_all.31.arrived_ref = f32[4,16,256]{2,1,0:T(8,128)S(1)} all-to-all(f32[4,16,256]{2,1,0:T(8,128)S(1)} %over_x.1), channel_id=1, replica_groups=mesh['zl'=4,'y'=4,'c'=2,'x'=4,'zh'=4] {'zh'}, dimensions={0} | all-to-all | bytes 131072 | tf_op jit(solution)/shard_map/all_to_all | solution.py:25
  55.4 6.8 %all_to_all.32.arrived_ref = f32[4,16,256]{2,1,0:T(8,128)S(1)} all-to-all(f32[4,16,256]{2,1,0:T(8,128)S(1)} %over_zh.1), channel_id=1, replica_groups=mesh['zl'=4,'y'=4,'c'=2,'x'=4,'zh'=4] {'x'}, dimensions={0} | all-to-all | bytes 131072 | tf_op jit(solution)/shard_map/all_to_all | solution.py:25
  62.3 6.4 %image_of_other.1 = (f32[16,40,128]{2,1,0:T(8,128)S(1)}, f32[16,1024]{1,0:T(8,128)S(1)}, bf16[32,1024]{1,0:T(8,128)(2,1)S(1)}, f32[8,128]{1,0:T(8,128)S(1)}) custom-call(f32[4,16,256]{2,1,0:T(8,128)S(1)} %all_to_all.32.arrived_ref, bf16[32,2,1024,256]{3,2,1,0:T(8,128)(2,1)} %get-tuple-element.12.matrix_hbm), custom_call_target="tpu_custom_call" | custom-call | flops 1073741824 | bytes 16777216 | tf_op jit(solution)/shard_map/image_of_other/pallas_call | solution.py:220
  68.7 6.6 %collective-permute-start = (f32[16,40,128]{2,1,0:T(8,128)S(1)}, f32[16,40,128]{2,1,0:T(8,128)S(1)}, u32[]{:S(2)}, u32[]{:S(2)}) collective-permute-start(f32[16,40,128]{2,1,0:T(8,128)S(1)} %get-tuple-element.15), channel_id=1, source_target_pairs={{0,16},{16,0},{1,17},{17,1},{2,18},{18,2},{3,19},{19,3},{4,20},{20... | collective-permute-start | bytes 983048 | tf_op jit(solution)/shard_map/ppermute | solution.py:29
  75.3 6.4 %image_of_own.1.own_ref = f32[16,40,128]{2,1,0:T(8,128)S(1)} custom-call(bf16[32,1024]{1,0:T(8,128)(2,1)S(1)} %get-tuple-element.13.left_ref, f32[8,128]{1,0:T(8,128)S(1)} %get-tuple-element.14.gram_ref, bf16[32,2,1024,256]{3,2,1,0:T(8,128)(2,1)} %get-tuple-element.12.matrix_hbm), custom_call_target="tpu_custom_call" | custom-call | flops 1073741824 | bytes 16777216 | tf_op jit(solution)/shard_map/image_of_own/pallas_call | solution.py:233
  81.7 0.0 collective-permute-done.other_ref
  81.7 16.7 %all_to_all.33.arrived_ref = f32[16,40,128]{2,1,0:T(8,128)S(1)} all-to-all(f32[16,40,128]{2,1,0:T(8,128)S(1)} %pair.1), channel_id=1, replica_groups=mesh['zl'=4,'y'=4,'c'=2,'x'=4,'zh'=4] {'zl','y'}, dimensions={0} | all-to-all | bytes 655360 | tf_op jit(solution)/shard_map/all_to_all | solution.py:25
  98.5 2.3 %factor.1 = (f32[16,32,128]{2,1,0:T(8,128)S(1)}, f32[16,1024]{1,0:T(8,128)}) custom-call(f32[16,40,128]{2,1,0:T(8,128)S(1)} %all_to_all.33.arrived_ref, f32[16,1024]{1,0:T(8,128)S(1)} %get-tuple-element.16.sketch_ref), custom_call_target="tpu_custom_call" | custom-call | tf_op jit(solution)/shard_map/factor/pallas_call | solution.py:294
  100.7 13.3 %all_to_all.34.own_ref.arrived_ref = f32[16,32,128]{2,1,0:T(8,128)S(1)} all-to-all(f32[16,32,128]{2,1,0:T(8,128)S(1)} %get-tuple-element.18), channel_id=1, replica_groups=mesh['zl'=4,'y'=4,'c'=2,'x'=4,'zh'=4] {'zl','y'}, dimensions={0} | all-to-all | bytes 524288 | tf_op jit(solution)/shard_map/all_to_all | solution.py:25
  114.0 1.2 square.1
  115.2 5.9 %all-to-all-start.5 = ((f32[32,8,128]{2,1,0:T(8,128)}), f32[32,8,128]{2,1,0:T(8,128)S(1)}, u32[]{:S(2)}, u32[]{:S(2)}) async-start(f32[32,8,128]{2,1,0:T(8,128)} %square.1), calls=%async_computation.5 | async-start | bytes 262144 | tf_op jit(solution)/shard_map/all_to_all | solution.py:25
  121.1 2.3 %collective-permute-start.1 = (f32[16,32,128]{2,1,0:T(8,128)S(1)}, f32[16,32,128]{2,1,0:T(8,128)S(1)}, u32[]{:S(2)}, u32[]{:S(2)}) collective-permute-start(f32[16,32,128]{2,1,0:T(8,128)S(1)} %all_to_all.34.own_ref.arrived_ref), channel_id=1, source_target_pairs={{0,16},{16,0},{1,17},{17,1},{2,18},{18,2},{3,19},{19,3},{4,20},{20... | collective-permute-start | bytes 786440 | tf_op jit(solution)/shard_map/ppermute | solution.py:29
  123.4 1.2 collective-permute-done.1.other_ref
  124.5 0.9 joined.1
  125.4 12.3 %all-to-all-done.5.arrived_ref = f32[32,8,128]{2,1,0:T(8,128)S(1)} async-done(((f32[32,8,128]{2,1,0:T(8,128)}), f32[32,8,128]{2,1,0:T(8,128)S(1)}, u32[]{:S(2)}, u32[]{:S(2)}) %all-to-all-start.5) | async-done | bytes 131104 | tf_op jit(solution)/shard_map/all_to_all | solution.py:25
  137.7 0.7 core.1
  (3 shorter events, 0.1 us)
Async XLA Ops:
  68.7 13.0 %collective-permute-start = (f32[16,40,128]{2,1,0:T(8,128)S(1)}, f32[16,40,128]{2,1,0:T(8,128)S(1)}, u32[]{:S(2)}, u32[]{:S(2)}) collective-permute-start(f32[16,40,128]{2,1,0:T(8,128)S(1)} %get-tuple-element.15), channel_id=1, source_target_pairs={{0,16},{16,0},{1,17},{17,1},{2,18},{18,2},{3,19},{19,3},{4,20},{20... | collective-permute-start | bytes 983048 | tf_op jit(solution)/shard_map/ppermute | solution.py:29
  115.2 22.5 %all-to-all-start.5 = ((f32[32,8,128]{2,1,0:T(8,128)}), f32[32,8,128]{2,1,0:T(8,128)S(1)}, u32[]{:S(2)}, u32[]{:S(2)}) async-start(f32[32,8,128]{2,1,0:T(8,128)} %square.1), calls=%async_computation.5 | async-start | bytes 262144 | tf_op jit(solution)/shard_map/all_to_all | solution.py:25
  121.1 3.4 %collective-permute-start.1 = (f32[16,32,128]{2,1,0:T(8,128)S(1)}, f32[16,32,128]{2,1,0:T(8,128)S(1)}, u32[]{:S(2)}, u32[]{:S(2)}) collective-permute-start(f32[16,32,128]{2,1,0:T(8,128)S(1)} %all_to_all.34.own_ref.arrived_ref), channel_id=1, source_target_pairs={{0,16},{16,0},{1,17},{17,1},{2,18},{18,2},{3,19},{19,3},{4,20},{20... | collective-permute-start | bytes 786440 | tf_op jit(solution)/shard_map/ppermute | solution.py:29

commit v4 on v3

--- a/solution.py
+++ b/solution.py
@@ -273,51 +273,74 @@
     return state[:, rank : 2 * rank]
 
 
-def factor_kernel(rows_total, arrived_ref, sketch_ref, share_ref, basis_ref):
+def share_kernel(arrived_ref, share_ref, gram_ref):
     total = jnp.sum(arrived_ref[...], axis=0)
+    height = share_ref.shape[1]
+    for copy in range(share_ref.shape[0]):
+        share_ref[copy] = total[:height]
+    gram_ref[...] = total[height:]
+
+
+def share_call(arrived):
+    peers, height, _ = arrived.shape
+    return pl.pallas_call(
+        share_kernel,
+        in_specs=[VMEM],
+        out_specs=[VMEM, VMEM],
+        out_shape=[
+            jax.ShapeDtypeStruct((peers, height - 8, LANES), F32),
+            jax.ShapeDtypeStruct((8, LANES), F32),
+        ],
+        compiler_params=SMALL,
+        name="share",
+    )(arrived)
+
+
+def factor_kernel(rows_total, gram_ref, sketch_ref, inverse_ref, basis_ref):
     rank = sketch_ref.shape[0]
-    height = total.shape[0] - 8
-    inverse = inverse_factor(unpacked(total[height:], rank) * (1.0 / rows_total))
-    for piece in range(0, height, rank):
-        part = jnp.dot(
-            inverse, total[piece : piece + rank], precision=HIGHEST, preferred_element_type=F32
-        )
-        for copy in range(share_ref.shape[0]):
-            share_ref[copy, piece : piece + rank, :] = part
+    inverse = inverse_factor(unpacked(gram_ref[...], rank) * (1.0 / rows_total))
+    inverse_ref[...] = inverse
     basis_ref[...] = jnp.dot(
         inverse, sketch_ref[...], precision=HIGHEST, preferred_element_type=F32
     )
 
 
-def factor_call(arrived, sketch, rows_total):
-    peers, height, _ = arrived.shape
+def factor_call(gram, sketch, rows_total):
+    rank = sketch.shape[0]
     return pl.pallas_call(
         functools.partial(factor_kernel, rows_total),
         in_specs=[VMEM, VMEM],
         out_specs=[VMEM, VMEM],
         out_shape=[
-            jax.ShapeDtypeStruct((peers, height - 8, LANES), F32),
+            jax.ShapeDtypeStruct((rank, rank), F32),
             jax.ShapeDtypeStruct(sketch.shape, F32),
         ],
         compiler_params=SMALL,
+        cost_estimate=pl.CostEstimate(
+            flops=1 << 30, bytes_accessed=8 << 20, transcendentals=0
+        ),
         name="factor",
-    )(arrived, sketch)
-
-
-def core_kernel(order, arrived_ref, core_ref):
-    total = jnp.sum(arrived_ref[...], axis=0)
-    core_ref[...] = unpacked(total, core_ref.shape[0]) * (1.0 / order)
-
-
-def core_call(arrived, rank, order):
+    )(gram, sketch)
+
+
+def core_kernel(order, arrived_ref, inverse_ref, core_ref):
+    square = unpacked(jnp.sum(arrived_ref[...], axis=0), core_ref.shape[0]) * (1.0 / order)
+    inverse = inverse_ref[...]
+    half = jnp.dot(inverse, square, precision=HIGHEST, preferred_element_type=F32)
+    core_ref[...] = lax.dot_general(
+        half, inverse, NT, precision=HIGHEST, preferred_element_type=F32
+    )
+
+
+def core_call(arrived, inverse, order):
     return pl.pallas_call(
         functools.partial(core_kernel, order),
-        in_specs=[VMEM],
-        out_specs=VMEM,
-        out_shape=jax.ShapeDtypeStruct((rank, rank), F32),
+        in_specs=[VMEM, VMEM],
+        out_specs=VMEM,
+        out_shape=jax.ShapeDtypeStruct(inverse.shape, F32),
         compiler_params=SMALL,
         name="core",
-    )(arrived)
+    )(arrived, inverse)
 
 
 def square_kernel(arrived_ref, square_ref):
@@ -347,28 +370,40 @@
     )(arrived)
 
 
-def joined_kernel(own_ref, other_ref, image_ref):
+def joined_kernel(own_ref, other_ref, inverse_ref, image_ref):
     core = lax.axis_index("c")
     rank = image_ref.shape[0]
     senders, height, _ = own_ref.shape
     pieces = height // rank
-    for sender in range(senders):
-        for ref, half in ((own_ref, core), (other_ref, 1 - core)):
-            for piece in range(pieces):
-                at = pl.multiple_of(((2 * sender + half) * pieces + piece) * LANES, LANES)
-                image_ref[:, pl.ds(at, LANES)] = ref[sender, piece * rank : (piece + 1) * rank, :]
-
-
-def joined_call(own, other, rank):
+    span = pieces * LANES
+    for ref, half in ((own_ref, core), (other_ref, 1 - core)):
+        raw = jnp.concatenate(
+            [
+                ref[sender, piece * rank : (piece + 1) * rank, :]
+                for sender in range(senders)
+                for piece in range(pieces)
+            ],
+            1,
+        )
+        image = jnp.dot(
+            inverse_ref[...], raw, precision=HIGHEST, preferred_element_type=F32
+        )
+        for sender in range(senders):
+            at = pl.multiple_of((2 * sender + half) * span, LANES)
+            image_ref[:, pl.ds(at, span)] = image[:, sender * span : (sender + 1) * span]
+
+
+def joined_call(own, other, inverse):
     senders, height, _ = own.shape
+    rank = inverse.shape[0]
     return pl.pallas_call(
         joined_kernel,
-        in_specs=[VMEM, VMEM],
+        in_specs=[VMEM, VMEM, VMEM],
         out_specs=VMEM,
         out_shape=jax.ShapeDtypeStruct((rank, 2 * senders * height // rank * LANES), F32),
         compiler_params=SMALL,
         name="joined",
-    )(own, other)
+    )(own, other, inverse)
 
 
 def shards(row_cells, col_cells, omega):
@@ -383,12 +418,13 @@
     over_both = resend_call(exchanged(over_x, "zh"), peers, "over_zh")
     first, second, sketch = image_calls(exchanged(over_both, "x"), matrix, 2)
     chip_parts = pair_call(second, swapped(first))
-    shares, basis = factor_call(exchanged(chip_parts, ("zl", "y")), sketch, rows_total)
+    shares, gram = share_call(exchanged(chip_parts, ("zl", "y")))
     own = exchanged(shares, ("zl", "y"))
+    inverse, basis = factor_call(gram, sketch, rows_total)
     other = swapped(own)
     square_parts = square_call(own, lax.axis_size(COL + ("c",)))
-    core = core_call(exchanged(square_parts, COL + ("c",)), rank, order)
-    image = joined_call(own, other, rank)
+    core = core_call(exchanged(square_parts, COL + ("c",)), inverse, order)
+    image = joined_call(own, other, inverse)
     return (basis, image, core)
 
 

time: 139 us -> 137 us (0.986)
  waiting for transfers between devices: 13.4 us -> 10.5 us
    all_to_all x1, waiting for transfers between devices: 12.3 us -> 10.5 us  [exchanged(): return lax.all_to_all(blocks, axes, split_axis=0, concat_axis=0, tiled=True)]
  transfers between devices with their start and end apart: 3 -> 3, of which waited for: 2 -> 1; matrix products, arithmetic and copies ran while one was open for 0% -> 0% of each run, Pallas kernels for 5% -> 7%
where the time goes in v4:
time: 137 us; the launch traced here: 136 us
  blocking collectives  72.6 us (53%)
  Pallas kernels  37.7 us (28%)
  starting transfers between devices  14.8 us (11%)
  waiting for transfers between devices  10.5 us (8%)
    all_to_all x5, blocking collectives, exchanged(): return lax.all_to_all(blocks, axes, split_axis=0, concat_axis=0, tiled=True)  72.6 us
    pallas_call x1, Pallas kernels, sketch_call(): pl.pallas_call(sketch_kernel, grid=(blocks // together,), in_specs=[pl.Bl...  19 us
    all_to_all x1, waiting for transfers between devices, exchanged(): return lax.all_to_all(blocks, axes, split_axis=0, concat_axis=0, tiled=True)  10.5 us
    ppermute x2, starting transfers between devices, swapped(): return lax.ppermute(block, 'c', [(0, 1), (1, 0)])  8.85 us
    pallas_call x1, Pallas kernels, image_calls(): pl.pallas_call(functools.partial(first_kernel, together), in_specs=[VMEM,...  6.4 us
    pallas_call x1, Pallas kernels, image_calls(): pl.pallas_call(functools.partial(second_kernel, together), in_specs=[VMEM...  6.39 us
    all_to_all x1, starting transfers between devices, exchanged(): return lax.all_to_all(blocks, axes, split_axis=0, concat_axis=0, tiled=True)  5.92 us
  transfers between devices with their start and end apart: 3, of which 1 were waited for; matrix products, arithmetic and copies ran while one was open for 0% of the time, Pallas kernels for 7%

profile of v4, /device:TPU:1, one launch (start us, length us, event | category | flops | bytes accessed | tf_op | source)
XLA Modules:
  0.0 136.4 jit_solution(7791878287681000889)
XLA Ops:
  0.6 19.0 %sketch.1 = (f32[4,16,256]{2,1,0:T(8,128)}, bf16[32,2,1024,256]{3,2,1,0:T(8,128)(2,1)}, f32[32,1024]{1,0:T(8,128)}) custom-call(s32[3,1024]{1,0:T(4,128)} %rows_ref.1, s32[3,8192]{1,0:T(4,128)} %cols_ref.1, f32[16,8192]{1,0:T(8,128)} %tests_ref.1), custom_call_target="tpu_custom_call" | custom-call | tf_op jit(solution)/shard_map/sketch/pallas_call | solution.py:96
  19.6 9.3 %all_to_all.30.arrived_ref = f32[4,16,256]{2,1,0:T(8,128)S(1)} all-to-all(f32[4,16,256]{2,1,0:T(8,128)} %get-tuple-element.13), channel_id=1, replica_groups=mesh['zl'=4,'y'=4,'c'=2,'x'=4,'zh'=4] {'x'}, dimensions={0} | all-to-all | bytes 131072 | tf_op jit(solution)/shard_map/all_to_all | solution.py:25
  28.9 26.5 %all_to_all.31.arrived_ref = f32[4,16,256]{2,1,0:T(8,128)S(1)} all-to-all(f32[4,16,256]{2,1,0:T(8,128)S(1)} %over_x.1), channel_id=1, replica_groups=mesh['zl'=4,'y'=4,'c'=2,'x'=4,'zh'=4] {'zh'}, dimensions={0} | all-to-all | bytes 131072 | tf_op jit(solution)/shard_map/all_to_all | solution.py:25
  55.4 6.8 %all_to_all.32.arrived_ref = f32[4,16,256]{2,1,0:T(8,128)S(1)} all-to-all(f32[4,16,256]{2,1,0:T(8,128)S(1)} %over_zh.1), channel_id=1, replica_groups=mesh['zl'=4,'y'=4,'c'=2,'x'=4,'zh'=4] {'x'}, dimensions={0} | all-to-all | bytes 131072 | tf_op jit(solution)/shard_map/all_to_all | solution.py:25
  62.3 6.4 %image_of_other.1 = (f32[16,40,128]{2,1,0:T(8,128)S(1)}, f32[16,1024]{1,0:T(8,128)S(1)}, bf16[32,1024]{1,0:T(8,128)(2,1)S(1)}, f32[8,128]{1,0:T(8,128)S(1)}) custom-call(f32[4,16,256]{2,1,0:T(8,128)S(1)} %all_to_all.32.arrived_ref, bf16[32,2,1024,256]{3,2,1,0:T(8,128)(2,1)} %get-tuple-element.14.matrix_hbm), custom_call_target="tpu_custom_call" | custom-call | flops 1073741824 | bytes 16777216 | tf_op jit(solution)/shard_map/image_of_other/pallas_call | solution.py:220
  68.7 6.6 %collective-permute-start = (f32[16,40,128]{2,1,0:T(8,128)S(1)}, f32[16,40,128]{2,1,0:T(8,128)S(1)}, u32[]{:S(2)}, u32[]{:S(2)}) collective-permute-start(f32[16,40,128]{2,1,0:T(8,128)S(1)} %get-tuple-element.17), channel_id=1, source_target_pairs={{0,16},{16,0},{1,17},{17,1},{2,18},{18,2},{3,19},{19,3},{4,20},{20... | collective-permute-start | bytes 983048 | tf_op jit(solution)/shard_map/ppermute | solution.py:29
  75.3 6.4 %image_of_own.1.own_ref = f32[16,40,128]{2,1,0:T(8,128)S(1)} custom-call(bf16[32,1024]{1,0:T(8,128)(2,1)S(1)} %get-tuple-element.15.left_ref, f32[8,128]{1,0:T(8,128)S(1)} %get-tuple-element.16.gram_ref, bf16[32,2,1024,256]{3,2,1,0:T(8,128)(2,1)} %get-tuple-element.14.matrix_hbm), custom_call_target="tpu_custom_call" | custom-call | flops 1073741824 | bytes 16777216 | tf_op jit(solution)/shard_map/image_of_own/pallas_call | solution.py:233
  81.7 0.0 collective-permute-done.other_ref
  81.7 16.7 %all_to_all.33.arrived_ref = f32[16,40,128]{2,1,0:T(8,128)S(1)} all-to-all(f32[16,40,128]{2,1,0:T(8,128)S(1)} %pair.1), channel_id=1, replica_groups=mesh['zl'=4,'y'=4,'c'=2,'x'=4,'zh'=4] {'zl','y'}, dimensions={0} | all-to-all | bytes 655360 | tf_op jit(solution)/shard_map/all_to_all | solution.py:25
  98.5 13.3 %all_to_all.34.own_ref.arrived_ref = f32[16,32,128]{2,1,0:T(8,128)S(1)} all-to-all(f32[16,32,128]{2,1,0:T(8,128)S(1)} %get-tuple-element.21), channel_id=1, replica_groups=mesh['zl'=4,'y'=4,'c'=2,'x'=4,'zh'=4] {'zl','y'}, dimensions={0} | all-to-all | bytes 524288 | tf_op jit(solution)/shard_map/all_to_all | solution.py:25
  111.8 1.2 square.1
  113.0 5.9 %all-to-all-start.5 = ((f32[32,8,128]{2,1,0:T(8,128)}), f32[32,8,128]{2,1,0:T(8,128)S(1)}, u32[]{:S(2)}, u32[]{:S(2)}) async-start(f32[32,8,128]{2,1,0:T(8,128)} %square.1), calls=%async_computation.5 | async-start | bytes 262144 | tf_op jit(solution)/shard_map/all_to_all | solution.py:25
  118.9 2.3 %collective-permute-start.1 = (f32[16,32,128]{2,1,0:T(8,128)S(1)}, f32[16,32,128]{2,1,0:T(8,128)S(1)}, u32[]{:S(2)}, u32[]{:S(2)}) collective-permute-start(f32[16,32,128]{2,1,0:T(8,128)S(1)} %all_to_all.34.own_ref.arrived_ref), channel_id=1, source_target_pairs={{0,16},{16,0},{1,17},{17,1},{2,18},{18,2},{3,19},{19,3},{4,20},{20... | collective-permute-start | bytes 786440 | tf_op jit(solution)/shard_map/ppermute | solution.py:29
  121.1 2.2 %factor.1 = (f32[16,16]{1,0:T(8,128)S(1)}, f32[16,1024]{1,0:T(8,128)}) custom-call(f32[8,128]{1,0:T(8,128)S(1)} %get-tuple-element.18.gram_ref, f32[16,1024]{1,0:T(8,128)S(1)} %get-tuple-element.19.sketch_ref), custom_call_target="tpu_custom_call" | custom-call | flops 1073741824 | bytes 8388608 | tf_op jit(solution)/shard_map/factor/pallas_call | solution.py:310
  123.4 0.0 collective-permute-done.1.other_ref
  123.4 1.5 %joined.1 = f32[16,8192]{1,0:T(8,128)} custom-call(f32[16,32,128]{2,1,0:T(8,128)S(1)} %all_to_all.34.own_ref.arrived_ref, f32[16,32,128]{2,1,0:T(8,128)S(1)} %collective-permute-done.1.other_ref, f32[16,16]{1,0:T(8,128)S(1)} %get-tuple-element.22.inverse_ref), custom_call_target="tpu_custom_call" | custom-call | tf_op jit(solution)/shard_map/joined/pallas_call | solution.py:399
  124.9 10.5 %all-to-all-done.5.arrived_ref = f32[32,8,128]{2,1,0:T(8,128)S(1)} async-done(((f32[32,8,128]{2,1,0:T(8,128)}), f32[32,8,128]{2,1,0:T(8,128)S(1)}, u32[]{:S(2)}, u32[]{:S(2)}) %all-to-all-start.5) | async-done | bytes 131104 | tf_op jit(solution)/shard_map/all_to_all | solution.py:25
  135.4 1.0 core.1
  (4 shorter events, 0.1 us)
Async XLA Ops:
  68.7 13.0 %collective-permute-start = (f32[16,40,128]{2,1,0:T(8,128)S(1)}, f32[16,40,128]{2,1,0:T(8,128)S(1)}, u32[]{:S(2)}, u32[]{:S(2)}) collective-permute-start(f32[16,40,128]{2,1,0:T(8,128)S(1)} %get-tuple-element.17), channel_id=1, source_target_pairs={{0,16},{16,0},{1,17},{17,1},{2,18},{18,2},{3,19},{19,3},{4,20},{20... | collective-permute-start | bytes 983048 | tf_op jit(solution)/shard_map/ppermute | solution.py:29
  113.0 22.5 %all-to-all-start.5 = ((f32[32,8,128]{2,1,0:T(8,128)}), f32[32,8,128]{2,1,0:T(8,128)S(1)}, u32[]{:S(2)}, u32[]{:S(2)}) async-start(f32[32,8,128]{2,1,0:T(8,128)} %square.1), calls=%async_computation.5 | async-start | bytes 262144 | tf_op jit(solution)/shard_map/all_to_all | solution.py:25
  118.9 4.5 %collective-permute-start.1 = (f32[16,32,128]{2,1,0:T(8,128)S(1)}, f32[16,32,128]{2,1,0:T(8,128)S(1)}, u32[]{:S(2)}, u32[]{:S(2)}) collective-permute-start(f32[16,32,128]{2,1,0:T(8,128)S(1)} %all_to_all.34.own_ref.arrived_ref), channel_id=1, source_target_pairs={{0,16},{16,0},{1,17},{17,1},{2,18},{18,2},{3,19},{19,3},{4,20},{20... | collective-permute-start | bytes 786440 | tf_op jit(solution)/shard_map/ppermute | solution.py:29

commit v5 on v4

--- a/solution.py
+++ b/solution.py
@@ -273,6 +273,29 @@
     return state[:, rank : 2 * rank]
 
 
+def flattened(square):
+    rank = square.shape[0]
+    side = LANES // rank
+    return jnp.concatenate(
+        [
+            jnp.concatenate([square[at + row : at + row + 1] for row in range(side)], 1)
+            for at in range(0, rank, side)
+        ],
+        0,
+    )
+
+
+def restored(flat, rank):
+    side = LANES // rank
+    return jnp.concatenate(
+        [
+            flat[row // side : row // side + 1, row % side * rank : (row % side + 1) * rank]
+            for row in range(rank)
+        ],
+        0,
+    )
+
+
 def share_kernel(arrived_ref, share_ref, gram_ref):
     total = jnp.sum(arrived_ref[...], axis=0)
     height = share_ref.shape[1]
@@ -324,7 +347,7 @@
 
 
 def core_kernel(order, arrived_ref, inverse_ref, core_ref):
-    square = unpacked(jnp.sum(arrived_ref[...], axis=0), core_ref.shape[0]) * (1.0 / order)
+    square = restored(jnp.sum(arrived_ref[...], axis=0), core_ref.shape[0]) * (1.0 / order)
     inverse = inverse_ref[...]
     half = jnp.dot(inverse, square, precision=HIGHEST, preferred_element_type=F32)
     core_ref[...] = lax.dot_general(
@@ -352,25 +375,27 @@
         for piece in range(2)
     ]
     image = jnp.concatenate(pieces, 1)
-    tile = packed(
+    flat = flattened(
         lax.dot_general(image, image, NT, precision=HIGHEST, preferred_element_type=F32)
     )
     for copy in range(square_ref.shape[0]):
-        square_ref[copy] = tile
+        square_ref[copy] = flat
 
 
 def square_call(arrived, copies):
+    rank = arrived.shape[1] // 2
     return pl.pallas_call(
         square_kernel,
         in_specs=[VMEM],
         out_specs=VMEM,
-        out_shape=jax.ShapeDtypeStruct((copies, 8, LANES), F32),
+        out_shape=jax.ShapeDtypeStruct((copies, rank * rank // LANES, LANES), F32),
         compiler_params=SMALL,
         name="square",
     )(arrived)
 
 
-def joined_kernel(own_ref, other_ref, inverse_ref, image_ref):
+def joined_kernel(own_ref, other_ref, inverse_ref, image_ref, same_ref):
+    same_ref[...] = inverse_ref[...]
     core = lax.axis_index("c")
     rank = image_ref.shape[0]
     senders, height, _ = own_ref.shape
@@ -399,8 +424,11 @@
     return pl.pallas_call(
         joined_kernel,
         in_specs=[VMEM, VMEM, VMEM],
-        out_specs=VMEM,
-        out_shape=jax.ShapeDtypeStruct((rank, 2 * senders * height // rank * LANES), F32),
+        out_specs=[VMEM, VMEM],
+        out_shape=[
+            jax.ShapeDtypeStruct((rank, 2 * senders * height // rank * LANES), F32),
+            jax.ShapeDtypeStruct(inverse.shape, F32),
+        ],
         compiler_params=SMALL,
         name="joined",
     )(own, other, inverse)
@@ -421,10 +449,10 @@
     shares, gram = share_call(exchanged(chip_parts, ("zl", "y")))
     own = exchanged(shares, ("zl", "y"))
     inverse, basis = factor_call(gram, sketch, rows_total)
-    other = swapped(own)
     square_parts = square_call(own, lax.axis_size(COL + ("c",)))
+    own, square_parts = lax.optimization_barrier((own, square_parts))
+    image, inverse = joined_call(own, swapped(own), inverse)
     core = core_call(exchanged(square_parts, COL + ("c",)), inverse, order)
-    image = joined_call(own, other, inverse)
     return (basis, image, core)
 
 

time: 137 us -> 137 us (level)
    all_to_all x1, starting transfers between devices: 5.92 us -> 3.66 us  [exchanged(): return lax.all_to_all(blocks, axes, split_axis=0, concat_axis=0, tiled=True)]
    ppermute x2, starting transfers between devices: 8.85 us -> 10.9 us  [swapped(): return lax.ppermute(block, 'c', [(0, 1), (1, 0)])]
where the time goes in v5:
time: 137 us; the launch traced here: 136 us
  blocking collectives  72.6 us (53%)
  Pallas kernels  37.7 us (28%)
  starting transfers between devices  14.6 us (11%)
  waiting for transfers between devices  10.7 us (8%)
    all_to_all x5, blocking collectives, exchanged(): return lax.all_to_all(blocks, axes, split_axis=0, concat_axis=0, tiled=True)  72.6 us
    pallas_call x1, Pallas kernels, sketch_call(): pl.pallas_call(sketch_kernel, grid=(blocks // together,), in_specs=[pl.Bl...  19 us
    ppermute x2, starting transfers between devices, swapped(): return lax.ppermute(block, 'c', [(0, 1), (1, 0)])  10.9 us
    all_to_all x1, waiting for transfers between devices, exchanged(): return lax.all_to_all(blocks, axes, split_axis=0, concat_axis=0, tiled=True)  10.7 us
    pallas_call x1, Pallas kernels, image_calls(): pl.pallas_call(functools.partial(first_kernel, together), in_specs=[VMEM,...  6.4 us
    pallas_call x1, Pallas kernels, image_calls(): pl.pallas_call(functools.partial(second_kernel, together), in_specs=[VMEM...  6.39 us
    all_to_all x1, starting transfers between devices, exchanged(): return lax.all_to_all(blocks, axes, split_axis=0, concat_axis=0, tiled=True)  3.66 us
  transfers between devices with their start and end apart: 3, of which 1 were waited for; matrix products, arithmetic and copies ran while one was open for 0% of the time, Pallas kernels for 7%

profile of v5, /device:TPU:1, one launch (start us, length us, event | category | flops | bytes accessed | tf_op | source)
XLA Modules:
  0.0 136.3 jit_solution(13336969005692720728)
XLA Ops:
  0.6 19.0 %sketch.1 = (f32[4,16,256]{2,1,0:T(8,128)}, bf16[32,2,1024,256]{3,2,1,0:T(8,128)(2,1)}, f32[32,1024]{1,0:T(8,128)}) custom-call(s32[3,1024]{1,0:T(4,128)} %rows_ref.1, s32[3,8192]{1,0:T(4,128)} %cols_ref.1, f32[16,8192]{1,0:T(8,128)} %tests_ref.1), custom_call_target="tpu_custom_call" | custom-call | tf_op jit(solution)/shard_map/sketch/pallas_call | solution.py:96
  19.6 9.3 %all_to_all.30.arrived_ref = f32[4,16,256]{2,1,0:T(8,128)S(1)} all-to-all(f32[4,16,256]{2,1,0:T(8,128)} %get-tuple-element.17), channel_id=1, replica_groups=mesh['zl'=4,'y'=4,'c'=2,'x'=4,'zh'=4] {'x'}, dimensions={0} | all-to-all | bytes 131072 | tf_op jit(solution)/shard_map/all_to_all | solution.py:25
  28.9 26.5 %all_to_all.31.arrived_ref = f32[4,16,256]{2,1,0:T(8,128)S(1)} all-to-all(f32[4,16,256]{2,1,0:T(8,128)S(1)} %over_x.1), channel_id=1, replica_groups=mesh['zl'=4,'y'=4,'c'=2,'x'=4,'zh'=4] {'zh'}, dimensions={0} | all-to-all | bytes 131072 | tf_op jit(solution)/shard_map/all_to_all | solution.py:25
  55.4 6.8 %all_to_all.32.arrived_ref = f32[4,16,256]{2,1,0:T(8,128)S(1)} all-to-all(f32[4,16,256]{2,1,0:T(8,128)S(1)} %over_zh.1), channel_id=1, replica_groups=mesh['zl'=4,'y'=4,'c'=2,'x'=4,'zh'=4] {'x'}, dimensions={0} | all-to-all | bytes 131072 | tf_op jit(solution)/shard_map/all_to_all | solution.py:25
  62.3 6.4 %image_of_other.1 = (f32[16,40,128]{2,1,0:T(8,128)S(1)}, f32[16,1024]{1,0:T(8,128)S(1)}, bf16[32,1024]{1,0:T(8,128)(2,1)S(1)}, f32[8,128]{1,0:T(8,128)S(1)}) custom-call(f32[4,16,256]{2,1,0:T(8,128)S(1)} %all_to_all.32.arrived_ref, bf16[32,2,1024,256]{3,2,1,0:T(8,128)(2,1)} %get-tuple-element.18.matrix_hbm), custom_call_target="tpu_custom_call" | custom-call | flops 1073741824 | bytes 16777216 | tf_op jit(solution)/shard_map/image_of_other/pallas_call | solution.py:220
  68.7 6.6 %collective-permute-start = (f32[16,40,128]{2,1,0:T(8,128)S(1)}, f32[16,40,128]{2,1,0:T(8,128)S(1)}, u32[]{:S(2)}, u32[]{:S(2)}) collective-permute-start(f32[16,40,128]{2,1,0:T(8,128)S(1)} %get-tuple-element.21), channel_id=1, source_target_pairs={{0,16},{16,0},{1,17},{17,1},{2,18},{18,2},{3,19},{19,3},{4,20},{20... | collective-permute-start | bytes 983048 | tf_op jit(solution)/shard_map/ppermute | solution.py:29
  75.3 6.4 %image_of_own.1.own_ref = f32[16,40,128]{2,1,0:T(8,128)S(1)} custom-call(bf16[32,1024]{1,0:T(8,128)(2,1)S(1)} %get-tuple-element.19.left_ref, f32[8,128]{1,0:T(8,128)S(1)} %get-tuple-element.20.gram_ref, bf16[32,2,1024,256]{3,2,1,0:T(8,128)(2,1)} %get-tuple-element.18.matrix_hbm), custom_call_target="tpu_custom_call" | custom-call | flops 1073741824 | bytes 16777216 | tf_op jit(solution)/shard_map/image_of_own/pallas_call | solution.py:233
  81.7 0.0 collective-permute-done.other_ref
  81.7 16.7 %all_to_all.33.arrived_ref = f32[16,40,128]{2,1,0:T(8,128)S(1)} all-to-all(f32[16,40,128]{2,1,0:T(8,128)S(1)} %pair.1), channel_id=1, replica_groups=mesh['zl'=4,'y'=4,'c'=2,'x'=4,'zh'=4] {'zl','y'}, dimensions={0} | all-to-all | bytes 655360 | tf_op jit(solution)/shard_map/all_to_all | solution.py:25
  98.5 13.3 %all_to_all.34.arrived_ref.own_ref = f32[16,32,128]{2,1,0:T(8,128)S(1)} all-to-all(f32[16,32,128]{2,1,0:T(8,128)S(1)} %get-tuple-element.25), channel_id=1, replica_groups=mesh['zl'=4,'y'=4,'c'=2,'x'=4,'zh'=4] {'zl','y'}, dimensions={0} | all-to-all | bytes 524288 | tf_op jit(solution)/shard_map/all_to_all | solution.py:25
  111.8 1.1 square.1
  112.9 4.3 %collective-permute-start.1 = (f32[16,32,128]{2,1,0:T(8,128)S(1)}, f32[16,32,128]{2,1,0:T(8,128)S(1)}, u32[]{:S(2)}, u32[]{:S(2)}) collective-permute-start(f32[16,32,128]{2,1,0:T(8,128)S(1)} %all_to_all.34.arrived_ref.own_ref), channel_id=1, source_target_pairs={{0,16},{16,0},{1,17},{17,1},{2,18},{18,2},{3,19},{19,3},{4,20},{20... | collective-permute-start | bytes 786440 | tf_op jit(solution)/shard_map/ppermute | solution.py:29
  117.2 3.7 %all-to-all-start.5 = ((f32[32,2,128]{2,1,0:T(2,128)}), f32[32,2,128]{2,1,0:T(2,128)S(1)}, u32[]{:S(2)}, u32[]{:S(2)}) async-start(f32[32,2,128]{2,1,0:T(2,128)} %square.1), calls=%async_computation.5 | async-start | bytes 65536 | tf_op jit(solution)/shard_map/all_to_all | solution.py:25
  120.9 2.2 %factor.1 = (f32[16,16]{1,0:T(8,128)S(1)}, f32[16,1024]{1,0:T(8,128)}) custom-call(f32[8,128]{1,0:T(8,128)S(1)} %get-tuple-element.22.gram_ref, f32[16,1024]{1,0:T(8,128)S(1)} %get-tuple-element.23.sketch_ref), custom_call_target="tpu_custom_call" | custom-call | flops 1073741824 | bytes 8388608 | tf_op jit(solution)/shard_map/factor/pallas_call | solution.py:333
  123.2 0.0 collective-permute-done.1.other_ref
  123.2 1.5 %joined.1 = (f32[16,8192]{1,0:T(8,128)}, f32[16,16]{1,0:T(8,128)S(1)}) custom-call(f32[16,32,128]{2,1,0:T(8,128)S(1)} %all_to_all.34.arrived_ref.own_ref, f32[16,32,128]{2,1,0:T(8,128)S(1)} %collective-permute-done.1.other_ref, f32[16,16]{1,0:T(8,128)S(1)} %get-tuple-element.27.inverse_ref), custom_call_target="tpu_custom_call" | custom-call | tf_op jit(solution)/shard_map/joined/pallas_call | solution.py:424
  124.7 10.7 %all-to-all-done.5.arrived_ref = f32[32,2,128]{2,1,0:T(2,128)S(1)} async-done(((f32[32,2,128]{2,1,0:T(2,128)}), f32[32,2,128]{2,1,0:T(2,128)S(1)}, u32[]{:S(2)}, u32[]{:S(2)}) %all-to-all-start.5) | async-done | bytes 32800 | tf_op jit(solution)/shard_map/all_to_all | solution.py:25
  135.3 1.0 core.1
  (4 shorter events, 0.1 us)
Async XLA Ops:
  68.7 13.0 %collective-permute-start = (f32[16,40,128]{2,1,0:T(8,128)S(1)}, f32[16,40,128]{2,1,0:T(8,128)S(1)}, u32[]{:S(2)}, u32[]{:S(2)}) collective-permute-start(f32[16,40,128]{2,1,0:T(8,128)S(1)} %get-tuple-element.21), channel_id=1, source_target_pairs={{0,16},{16,0},{1,17},{17,1},{2,18},{18,2},{3,19},{19,3},{4,20},{20... | collective-permute-start | bytes 983048 | tf_op jit(solution)/shard_map/ppermute | solution.py:29
  112.9 10.2 %collective-permute-start.1 = (f32[16,32,128]{2,1,0:T(8,128)S(1)}, f32[16,32,128]{2,1,0:T(8,128)S(1)}, u32[]{:S(2)}, u32[]{:S(2)}) collective-permute-start(f32[16,32,128]{2,1,0:T(8,128)S(1)} %all_to_all.34.arrived_ref.own_ref), channel_id=1, source_target_pairs={{0,16},{16,0},{1,17},{17,1},{2,18},{18,2},{3,19},{19,3},{4,20},{20... | collective-permute-start | bytes 786440 | tf_op jit(solution)/shard_map/ppermute | solution.py:29
  117.2 18.1 %all-to-all-start.5 = ((f32[32,2,128]{2,1,0:T(2,128)}), f32[32,2,128]{2,1,0:T(2,128)S(1)}, u32[]{:S(2)}, u32[]{:S(2)}) async-start(f32[32,2,128]{2,1,0:T(2,128)} %square.1), calls=%async_computation.5 | async-start | bytes 65536 | tf_op jit(solution)/shard_map/all_to_all | solution.py:25
